TPU v7x, 512 devices: a whole 4x4x16 slice. The times are simulated.
512 devices in a mesh: ctx: 32 (over x_hi, z), fsdp: 16 (over y, x_lo, core).
Axes of the slice: x: 4 (x_hi: 2, x_lo: 2; x = x_hi * 2 + x_lo), y: 4, z: 16, core: 2. Of those that a mesh axis runs over, the one named last changes fastest.
Arguments:
- streams: bfloat16 [3, 16384, 8192], P(None, ('ctx', 'fsdp')), may hold values from -6 to 6
- segments: int32 [16384], replicated, may hold values from 0 to 63, never falling along the last dimension, each value on 1 to 4096 neighbouring positions
- short_taps: float32 [3, 3, 8192], P(None, None, 'fsdp'), may hold values from -3 to 3
- decay_rates: float32 [512, 16], P('fsdp'), may hold values from 1.2207031e-05 to 0.1
- residues: float32 [512, 16], P('fsdp'), may hold values from -2 to 2
- skip_gain: float32 [8192], P('fsdp'), may hold values from -4 to 4
Outputs:
- output: bfloat16 [16384, 8192], P(('ctx', 'fsdp'))
Inputs may be any that keep to these rules, and one draw needn't show every extreme that they name: `segments`: never falling along the window; every document has 1 to 4096 tokens and one has exactly 4096.
All inputs are finite; a program needn't handle non-finite values.
Results may differ from a plain program's by a relative error of at most 0.0064.
Values may be sent and summed in bfloat16 or wider, within the bound.
A program may use at most 64 MiB of HBM per device.

v0:
```python
import jax
import jax.numpy as jnp
from jax import lax
from jax.sharding import PartitionSpec as P

GROUP = 16
MODES = 16
SHORT = 3
SPAN = 8


def shifted_2(block, axis, distance):
    devices = range(lax.axis_size(axis))
    route = [(i - distance, i) for i in devices if i - distance in devices]
    return lax.ppermute(block, axis, route)


def contract(pattern, left_side, right_side):
    return jnp.einsum(pattern, left_side, right_side, precision=lax.Precision.HIGHEST)


def featurize(block_rows, before_rows, tap_rows, row_marks, before_marks):
    margin = before_rows.shape[1]
    row_count = block_rows.shape[1]
    joined = jnp.concatenate([before_rows, block_rows], axis=1)
    all_marks = jnp.concatenate([before_marks, row_marks])
    summed = block_rows.astype(jnp.float32) * tap_rows[:, 0][:, None, :]
    for offset in range(1, margin + 1):
        shifted = joined[:, margin - offset : margin - offset + row_count].astype(jnp.float32)
        agreeing = all_marks[margin - offset : margin - offset + row_count] == row_marks
        summed = (
            summed
            + jnp.where(agreeing[None, :, None], shifted, 0.0) * tap_rows[:, offset][:, None, :]
        )
    queries = summed[0].astype(jnp.bfloat16)
    gated_prod = (summed[1] * summed[2]).astype(jnp.bfloat16)
    return lax.optimization_barrier((queries, gated_prod))


def tile_filter(gated_prod, tile_marks, decay_rates, mode_gain, rising):
    tile_rows, channels = gated_prod.shape
    groups = channels // GROUP
    block_len = min(128, tile_rows)
    offsets = jnp.arange(block_len, dtype=jnp.float32)
    forward = mode_gain[:, :, None] * jnp.exp(-decay_rates[:, :, None] * offsets)
    backward = jnp.exp(decay_rates[:, :, None] * offsets)
    causal = (offsets[:, None] >= offsets[None, :]).astype(jnp.float32)
    kernel = contract("gmt,gms->gts", forward, backward) * causal
    mode_rates = decay_rates.T[:, :, None]
    closing = jnp.exp(-mode_rates * (block_len - 1.0 - offsets))
    through = jnp.exp(-mode_rates * block_len)
    head_rising = rising[:, :, :block_len]
    values = gated_prod.astype(jnp.float32).reshape(tile_rows, groups, GROUP)
    carried = jnp.zeros((MODES, groups, GROUP), jnp.float32)
    last_seen = jnp.int32(-1)
    pieces = []
    for number in range(tile_rows // block_len):
        block_vals = values[number * block_len : (number + 1) * block_len]
        block_marks = tile_marks[number * block_len : (number + 1) * block_len]
        agreeing = (block_marks[:, None] == block_marks[None, :]).astype(jnp.float32)
        inside = contract("gts,sgc->tgc", kernel * agreeing, block_vals)
        follow = (block_marks == last_seen).astype(jnp.float32)
        inside = inside + follow[:, None, None] * contract("mgt,mgc->tgc", head_rising, carried)
        ending = (block_marks == block_marks[block_len - 1]).astype(jnp.float32)
        fresh_state = contract("mgs,sgc->mgc", closing * ending, block_vals)
        passing = (block_marks[block_len - 1] == last_seen).astype(jnp.float32)
        carried = fresh_state + passing * through * carried
        last_seen = block_marks[block_len - 1]
        pieces.append(inside)
    return (jnp.concatenate(pieces, axis=0), carried)


def local(streams, segments, short_taps, decay_rates, residues, skip_gain):
    fsdp_count = lax.axis_size("fsdp")
    ctx_count = lax.axis_size("ctx")
    tile_index = lax.axis_index("ctx")
    own_rows = streams.shape[1]
    tile_rows = own_rows * fsdp_count
    margin = SHORT - 1
    padded_marks = jnp.concatenate([jnp.full((margin,), -1, jnp.int32), segments])
    tile_start = tile_index * tile_rows
    tile_marks = lax.dynamic_slice_in_dim(segments, tile_start, tile_rows)
    local_streams = lax.all_to_all(streams, "fsdp", split_axis=2, concat_axis=1, tiled=True)
    before_rows = shifted_2(local_streams[:, tile_rows - margin :, :], "ctx", 1)
    before_marks = lax.dynamic_slice_in_dim(padded_marks, tile_start, margin)
    queries, gated_prod = featurize(
        local_streams, before_rows, short_taps, tile_marks, before_marks
    )
    channels = gated_prod.shape[1]
    groups = channels // GROUP
    mode_gain = residues * jnp.sqrt(-jnp.expm1(-2.0 * decay_rates))
    positions = jnp.arange(tile_rows, dtype=jnp.float32)
    mode_rates = decay_rates.T[:, :, None]
    rising = mode_gain.T[:, :, None] * jnp.exp(-mode_rates * (positions + 1.0))
    local_part, end_state = tile_filter(gated_prod, tile_marks, decay_rates, mode_gain, rising)
    first_mark = tile_marks[0]
    falling = jnp.exp(-mode_rates * (tile_rows - 1.0 - positions))

    def source_state(operand):
        source_vals, source_marks = operand
        chosen = (source_marks == first_mark).astype(jnp.float32)
        return contract(
            "mgs,sgc->mgc",
            falling * chosen,
            source_vals.astype(jnp.float32).reshape(tile_rows, groups, GROUP),
        )

    def empty_state(operand):
        return jnp.zeros((MODES, groups, GROUP), jnp.float32)

    prior_state = jnp.zeros((MODES, groups, GROUP), jnp.float32)
    for distance in range(1, min(SPAN, ctx_count - 1) + 1):
        source_tile = shifted_2(gated_prod, "ctx", distance)
        source_index = tile_index - distance
        source_marks = lax.dynamic_slice_in_dim(
            segments, jnp.maximum(source_index, 0) * tile_rows, tile_rows
        )
        paired = (source_index >= 0) & (source_marks[tile_rows - 1] == first_mark)
        received = lax.cond(paired, source_state, empty_state, (source_tile, source_marks))
        prior_state = prior_state + jnp.exp(-mode_rates * ((distance - 1) * tile_rows)) * received
    prior_mark = first_mark.astype(jnp.float32)
    follow_tile = (tile_marks.astype(jnp.float32) == prior_mark).astype(jnp.float32)
    filtered = local_part + follow_tile[:, None, None] * contract(
        "mgt,mgc->tgc", rising, prior_state
    )
    mixed_out = (
        filtered.reshape(tile_rows, channels) + skip_gain * gated_prod.astype(jnp.float32)
    ).astype(jnp.bfloat16)
    mixed_out = lax.optimization_barrier(mixed_out)
    payload = (queries.astype(jnp.float32) * mixed_out.astype(jnp.float32)).astype(jnp.bfloat16)
    returned = lax.all_to_all(payload, "fsdp", split_axis=0, concat_axis=1, tiled=True)
    return returned


def solution(mesh):
    placed = (
        P(None, ("ctx", "fsdp"), None),
        P(),
        P(None, None, "fsdp"),
        P("fsdp", None),
        P("fsdp", None),
        P("fsdp"),
    )
    return jax.shard_map(
        local, mesh=mesh, in_specs=placed, out_specs=P(("ctx", "fsdp"), None), check_vma=False
    )
```

profile of v0, /device:TPU:7, one launch (start us, length us, event | category | flops | bytes accessed | tf_op | source)
XLA Modules:
  0.0 510.8 jit_solution(597949325799028393)
XLA Ops:
  0.0 10.6 %copy.91 = bf16[3,32,8192]{1,0,2:T(4,128)(2,1)} copy(bf16[3,32,8192]{2,1,0:T(8,128)(2,1)} %param.22) | data formatting | bytes 3145728 | tf_op args[0]
  10.6 13.2 %reshape.234 = bf16[16,2,24576]{2,1,0:T(2,128)(2,1)} reshape(bf16[8192,3,32]{2,1,0:T(4,128)(2,1)} %bitcast.120) | data formatting | bytes 3145728
  23.8 6.4 %all-to-all-start = ((bf16[16,2,24576]{2,1,0:T(2,128)(2,1)}), bf16[16,2,24576]{2,1,0:T(2,128)(2,1)}, u32[]{:S(2)}, u32[]{:S(2)}) async-start(bf16[16,2,24576]{2,1,0:T(2,128)(2,1)} %reshape.234), calls=%async_computation | async-start | bytes 3145728 | tf_op jit(solution)/shard_map/all_to_all | solution.py:83
  34.2 2.5 compare_convert_fusion.18
  40.5 1.0 copy-done
  41.5 1.0 convolution_multiply_fusion.4
  42.6 3.7 fusion.87
  46.2 5.1 all-to-all-done
  51.3 12.6 %reshape.235 = bf16[8192,3,32]{2,1,0:T(4,128)(2,1)} reshape(bf16[16,2,24576]{2,1,0:T(2,128)(2,1)} %all-to-all-done) | data formatting | bytes 3145728
  63.9 11.8 %copy.128 = bf16[3,32,16,512]{3,1,2,0:T(8,128)(2,1)} copy(bf16[3,32,16,512]{1,0,3,2:T(4,128)(2,1)} %bitcast.119) | data formatting | bytes 3145728 | tf_op jit(solution)/shard_map/all_to_all | solution.py:83
  76.4 3.5 collective-permute-start
  102.8 3.9 multiply_add_fusion
  106.7 0.9 fusion.67
  107.6 0.9 fusion.68
  108.5 1.8 fusion.125
  110.4 14.5 %collective-permute-start.8 = (bf16[512,512]{1,0:T(8,128)(2,1)}, bf16[512,512]{1,0:T(8,128)(2,1)}, u32[]{:S(2)}, u32[]{:S(2)}) collective-permute-start(bf16[512,512]{1,0:T(8,128)(2,1)} %fusion.68), channel_id=1, source_target_pairs={{0,128},{16,144},{32,160},{48,176},{64,192},{80,208},{96,224},{112... | collective-permute-start | bytes 1572872 | tf_op jit(solution)/shard_map/ppermute | solution.py:15
  124.9 4.0 collective-permute-start.7
  128.9 2.8 collective-permute-start.6
  131.8 1.9 collective-permute-start.5
  133.7 2.1 collective-permute-start.4
  135.9 1.0 copy.100
  137.0 1.7 copy.94
  138.6 1.7 copy.105
  140.3 1.4 fusion.57
  141.7 1.3 convolution_multiply_fusion.3
  143.1 1.2 fusion.56
  144.3 1.0 convolution_multiply_fusion.2
  145.2 2.5 fusion.40
  147.7 2.5 fusion.46
  150.7 2.5 fusion.34
  153.2 12.9 %collective-permute-start.3 = (bf16[512,512]{1,0:T(8,128)(2,1)}, bf16[512,512]{1,0:T(8,128)(2,1)}, u32[]{:S(2)}, u32[]{:S(2)}) collective-permute-start(bf16[512,512]{1,0:T(8,128)(2,1)} %fusion.68), channel_id=1, source_target_pairs={{0,48},{16,64},{32,80},{48,96},{64,112},{80,128},{96,144},{112,160... | collective-permute-start | bytes 1572872 | tf_op jit(solution)/shard_map/ppermute | solution.py:15
  166.0 106.9 %collective-permute-done.7 = bf16[512,512]{1,0:T(8,128)(2,1)} collective-permute-done((bf16[512,512]{1,0:T(8,128)(2,1)}, bf16[512,512]{1,0:T(8,128)(2,1)}, u32[]{:S(2)}, u32[]{:S(2)}) %collective-permute-start.7) | collective-permute-done | bytes 524320 | tf_op jit(solution)/shard_map/ppermute | solution.py:15
  272.9 1.9 collective-permute-start.2
  274.9 25.4 %collective-permute-done.6 = bf16[512,512]{1,0:T(8,128)(2,1)} collective-permute-done((bf16[512,512]{1,0:T(8,128)(2,1)}, bf16[512,512]{1,0:T(8,128)(2,1)}, u32[]{:S(2)}, u32[]{:S(2)}) %collective-permute-start.6) | collective-permute-done | bytes 524320 | tf_op jit(solution)/shard_map/ppermute | solution.py:15
  300.3 41.9 %collective-permute-start.1 = (bf16[512,512]{1,0:T(8,128)(2,1)}, bf16[512,512]{1,0:T(8,128)(2,1)}, u32[]{:S(2)}, u32[]{:S(2)}) collective-permute-start(bf16[512,512]{1,0:T(8,128)(2,1)} %fusion.68), channel_id=1, source_target_pairs={{0,16},{16,32},{32,48},{48,64},{64,80},{80,96},{96,112},{112,128},... | collective-permute-start | bytes 1572872 | tf_op jit(solution)/shard_map/ppermute | solution.py:15
  342.6 2.5 fusion.52
  345.9 5.3 %collective-permute-done.5 = bf16[512,512]{1,0:T(8,128)(2,1)} collective-permute-done((bf16[512,512]{1,0:T(8,128)(2,1)}, bf16[512,512]{1,0:T(8,128)(2,1)}, u32[]{:S(2)}, u32[]{:S(2)}) %collective-permute-start.5) | collective-permute-done | bytes 524320 | tf_op jit(solution)/shard_map/ppermute | solution.py:15
  351.2 85.5 %collective-permute-done.4 = bf16[512,512]{1,0:T(8,128)(2,1)} collective-permute-done((bf16[512,512]{1,0:T(8,128)(2,1)}, bf16[512,512]{1,0:T(8,128)(2,1)}, u32[]{:S(2)}, u32[]{:S(2)}) %collective-permute-start.4) | collective-permute-done | bytes 524320 | tf_op jit(solution)/shard_map/ppermute | solution.py:15
  437.0 38.5 %collective-permute-done.2 = bf16[512,512]{1,0:T(8,128)(2,1)} collective-permute-done((bf16[512,512]{1,0:T(8,128)(2,1)}, bf16[512,512]{1,0:T(8,128)(2,1)}, u32[]{:S(2)}, u32[]{:S(2)}) %collective-permute-start.2) | collective-permute-done | bytes 524320 | tf_op jit(solution)/shard_map/ppermute | solution.py:15
  475.7 11.2 %collective-permute-done.1 = bf16[512,512]{1,0:T(8,128)(2,1)} collective-permute-done((bf16[512,512]{1,0:T(8,128)(2,1)}, bf16[512,512]{1,0:T(8,128)(2,1)}, u32[]{:S(2)}, u32[]{:S(2)}) %collective-permute-start.1) | collective-permute-done | bytes 524320 | tf_op jit(solution)/shard_map/ppermute | solution.py:15
  486.9 4.0 conditional.8
  486.9 1.3 copy.108
  488.2 1.3 compare_convert_fusion
  489.5 1.5 convolution_bitcast_fusion
  491.0 3.3 fusion.30
  495.0 1.2 add_convert_fusion
  496.3 13.6 %all_to_all.37 = bf16[16,32,512]{2,1,0:T(8,128)(2,1)S(1)} all-to-all(bf16[16,32,512]{2,1,0:T(8,128)(2,1)S(1)} %bitcast.124), channel_id=1, replica_groups=mesh['ctx'=32,'fsdp'=16] {'fsdp'}, dimensions={0} | all-to-all | bytes 1048576 | tf_op jit(solution)/shard_map/all_to_all | solution.py:131
  509.9 0.8 copy.132
  (152 shorter events, 20.3 us)
Async XLA Ops:
  23.8 6.4 %copy-start.11 = (s32[16384]{0:T(1024)S(1)}, s32[16384]{0:T(1024)}, u32[]{:S(2)}) copy-start(s32[16384]{0:T(1024)} %param.23) | copy-start | bytes 196612
  23.8 13.0 %copy-start.22 = (f32[3,3,512]{2,1,0:T(4,128)S(1)}, f32[3,3,512]{2,1,0:T(4,128)}, u32[]{:S(2)}) copy-start(f32[3,3,512]{2,1,0:T(4,128)} %param.24) | copy-start | bytes 55300
  23.8 14.4 %copy-start.12 = (f32[32,16]{0,1:T(8,128)S(1)}, f32[32,16]{0,1:T(8,128)}, u32[]{:S(2)}) copy-start(f32[32,16]{0,1:T(8,128)} %param.25) | copy-start | bytes 6148
  23.8 14.4 %copy-start.23 = (f32[32,16]{0,1:T(8,128)S(1)}, f32[32,16]{0,1:T(8,128)}, u32[]{:S(2)}) copy-start(f32[32,16]{0,1:T(8,128)} %param.26) | copy-start | bytes 6148
  23.8 27.5 %all-to-all-start = ((bf16[16,2,24576]{2,1,0:T(2,128)(2,1)}), bf16[16,2,24576]{2,1,0:T(2,128)(2,1)}, u32[]{:S(2)}, u32[]{:S(2)}) async-start(bf16[16,2,24576]{2,1,0:T(2,128)(2,1)} %reshape.234), calls=%async_computation | async-start | bytes 3145728 | tf_op jit(solution)/shard_map/all_to_all | solution.py:83
  30.3 52.2 %copy-start.37 = (s32[512]{0:T(512)}, s32[512]{0:T(512)S(1)}, u32[]{:S(2)}) copy-start(s32[512]{0:T(512)S(1)} %get-tuple-element.236) | copy-start | bytes 6148
  30.3 54.1 %copy-start.35 = (s32[512]{0:T(512)}, s32[512]{0:T(512)S(1)}, u32[]{:S(2)}) copy-start(s32[512]{0:T(512)S(1)} %get-tuple-element.237) | copy-start | bytes 6148
  30.3 55.9 %copy-start.33 = (s32[512]{0:T(512)}, s32[512]{0:T(512)S(1)}, u32[]{:S(2)}) copy-start(s32[512]{0:T(512)S(1)} %get-tuple-element.230) | copy-start | bytes 6148
  30.3 57.8 %copy-start.31 = (s32[512]{0:T(512)}, s32[512]{0:T(512)S(1)}, u32[]{:S(2)}) copy-start(s32[512]{0:T(512)S(1)} %get-tuple-element.231) | copy-start | bytes 6148
  30.3 59.6 %copy-start.29 = (s32[512]{0:T(512)}, s32[512]{0:T(512)S(1)}, u32[]{:S(2)}) copy-start(s32[512]{0:T(512)S(1)} %get-tuple-element.232) | copy-start | bytes 6148
  30.4 61.5 %copy-start.27 = (s32[512]{0:T(512)}, s32[512]{0:T(512)S(1)}, u32[]{:S(2)}) copy-start(s32[512]{0:T(512)S(1)} %get-tuple-element.233) | copy-start | bytes 6148
  30.4 63.3 %copy-start.25 = (s32[512]{0:T(512)}, s32[512]{0:T(512)S(1)}, u32[]{:S(2)}) copy-start(s32[512]{0:T(512)S(1)} %get-tuple-element.234) | copy-start | bytes 6148
  30.4 65.2 %copy-start.24 = (s32[512]{0:T(512)}, s32[512]{0:T(512)S(1)}, u32[]{:S(2)}) copy-start(s32[512]{0:T(512)S(1)} %get-tuple-element.229) | copy-start | bytes 6148
  38.3 7.9 %copy-start.21 = (f32[512]{0:T(512)}, f32[512]{0:T(512)S(1)}, u32[]{:S(2)}) copy-start(f32[512]{0:T(512)S(1)} %iota_add_fusion) | copy-start | bytes 6148
  38.6 7.6 %copy-start.9 = (f32[16,32]{0,1:T(8,128)}, f32[16,32]{0,1:T(8,128)S(1)}, u32[]{:S(2)}) copy-start(f32[16,32]{0,1:T(8,128)S(1)} %copy.98) | copy-start | bytes 6148
  63.9 38.9 %copy-start.40 = (pred[512]{0:T(512)(128)(4,1)S(1)}, pred[512]{0:T(512)(128)(4,1)}, u32[]{:S(2)}) copy-start(pred[512]{0:T(512)(128)(4,1)} %get-tuple-element.258) | copy-start | bytes 1540
  76.4 26.4 %collective-permute-start = (bf16[3,2,512]{2,1,0:T(2,128)(2,1)S(1)}, bf16[3,2,512]{2,1,0:T(2,128)(2,1)S(1)}, u32[]{:S(2)}, u32[]{:S(2)}) collective-permute-start(bf16[3,2,512]{2,1,0:T(2,128)(2,1)S(1)} %slice.154), channel_id=1, source_target_pairs={{0,16},{16,32},{32,48},{48,64},{64,80},{80,96},{96,112},{112,128},... | collective-permute-start | bytes 18440 | tf_op jit(solution)/shard_map/ppermute | solution.py:15
  110.4 42.8 %collective-permute-start.8 = (bf16[512,512]{1,0:T(8,128)(2,1)}, bf16[512,512]{1,0:T(8,128)(2,1)}, u32[]{:S(2)}, u32[]{:S(2)}) collective-permute-start(bf16[512,512]{1,0:T(8,128)(2,1)} %fusion.68), channel_id=1, source_target_pairs={{0,128},{16,144},{32,160},{48,176},{64,192},{80,208},{96,224},{112... | collective-permute-start | bytes 1572872 | tf_op jit(solution)/shard_map/ppermute | solution.py:15
  124.9 148.0 %collective-permute-start.7 = (bf16[512,512]{1,0:T(8,128)(2,1)}, bf16[512,512]{1,0:T(8,128)(2,1)}, u32[]{:S(2)}, u32[]{:S(2)}) collective-permute-start(bf16[512,512]{1,0:T(8,128)(2,1)} %fusion.68), channel_id=1, source_target_pairs={{0,112},{16,128},{32,144},{48,160},{64,176},{80,192},{96,208},{112... | collective-permute-start | bytes 1572872 | tf_op jit(solution)/shard_map/ppermute | solution.py:15
  128.9 171.4 %collective-permute-start.6 = (bf16[512,512]{1,0:T(8,128)(2,1)}, bf16[512,512]{1,0:T(8,128)(2,1)}, u32[]{:S(2)}, u32[]{:S(2)}) collective-permute-start(bf16[512,512]{1,0:T(8,128)(2,1)} %fusion.68), channel_id=1, source_target_pairs={{0,96},{16,112},{32,128},{48,144},{64,160},{80,176},{96,192},{112,... | collective-permute-start | bytes 1572872 | tf_op jit(solution)/shard_map/ppermute | solution.py:15
  131.8 219.4 %collective-permute-start.5 = (bf16[512,512]{1,0:T(8,128)(2,1)}, bf16[512,512]{1,0:T(8,128)(2,1)}, u32[]{:S(2)}, u32[]{:S(2)}) collective-permute-start(bf16[512,512]{1,0:T(8,128)(2,1)} %fusion.68), channel_id=1, source_target_pairs={{0,80},{16,96},{32,112},{48,128},{64,144},{80,160},{96,176},{112,1... | collective-permute-start | bytes 1572872 | tf_op jit(solution)/shard_map/ppermute | solution.py:15
  133.7 303.0 %collective-permute-start.4 = (bf16[512,512]{1,0:T(8,128)(2,1)}, bf16[512,512]{1,0:T(8,128)(2,1)}, u32[]{:S(2)}, u32[]{:S(2)}) collective-permute-start(bf16[512,512]{1,0:T(8,128)(2,1)} %fusion.68), channel_id=1, source_target_pairs={{0,64},{16,80},{32,96},{48,112},{64,128},{80,144},{96,160},{112,17... | collective-permute-start | bytes 1572872 | tf_op jit(solution)/shard_map/ppermute | solution.py:15
  140.3 4.0 copy-start.1
  140.3 4.9 copy-start.8
  143.0 4.7 copy-start.7
  147.7 2.5 copy-start.42
  147.7 2.5 copy-start.43
  147.7 2.9 copy-start.3
  147.7 3.0 copy-start.5
  147.7 3.0 copy-start.6
  150.2 192.0 %copy-start.41 = (f32[128]{0:T(128)S(1)}, f32[128]{0:T(128)}, u32[]{:S(2)}) copy-start(f32[128]{0:T(128)} %get-tuple-element.274) | copy-start | bytes 1540
  150.2 192.4 %copy-start.4 = (bf16[128,512]{0,1:T(8,128)(2,1)S(1)}, bf16[128,512]{0,1:T(8,128)(2,1)}, u32[]{:S(2)}) copy-start(bf16[128,512]{0,1:T(8,128)(2,1)} %copy.105) | copy-start | bytes 393220
  153.1 192.0 %copy-start.38 = (s32[512]{0:T(512)S(1)}, s32[512]{0:T(512)}, u32[]{:S(2)}) copy-start(s32[512]{0:T(512)} %copy-done.37) | copy-start | bytes 6148
  153.2 283.8 %collective-permute-start.3 = (bf16[512,512]{1,0:T(8,128)(2,1)}, bf16[512,512]{1,0:T(8,128)(2,1)}, u32[]{:S(2)}, u32[]{:S(2)}) collective-permute-start(bf16[512,512]{1,0:T(8,128)(2,1)} %fusion.68), channel_id=1, source_target_pairs={{0,48},{16,64},{32,80},{48,96},{64,112},{80,128},{96,144},{112,160... | collective-permute-start | bytes 1572872 | tf_op jit(solution)/shard_map/ppermute | solution.py:15
  272.9 202.6 %collective-permute-start.2 = (bf16[512,512]{1,0:T(8,128)(2,1)}, bf16[512,512]{1,0:T(8,128)(2,1)}, u32[]{:S(2)}, u32[]{:S(2)}) collective-permute-start(bf16[512,512]{1,0:T(8,128)(2,1)} %fusion.68), channel_id=1, source_target_pairs={{0,32},{16,48},{32,64},{48,80},{64,96},{80,112},{96,128},{112,144}... | collective-permute-start | bytes 1572872 | tf_op jit(solution)/shard_map/ppermute | solution.py:15
  300.3 186.6 %collective-permute-start.1 = (bf16[512,512]{1,0:T(8,128)(2,1)}, bf16[512,512]{1,0:T(8,128)(2,1)}, u32[]{:S(2)}, u32[]{:S(2)}) collective-permute-start(bf16[512,512]{1,0:T(8,128)(2,1)} %fusion.68), channel_id=1, source_target_pairs={{0,16},{16,32},{32,48},{48,64},{64,80},{80,96},{96,112},{112,128},... | collective-permute-start | bytes 1572872 | tf_op jit(solution)/shard_map/ppermute | solution.py:15
  345.8 5.3 %copy-start.32 = (s32[512]{0:T(512)S(1)}, s32[512]{0:T(512)}, u32[]{:S(2)}) copy-start(s32[512]{0:T(512)} %copy-done.31) | copy-start | bytes 6148
  345.9 90.8 %copy-start.30 = (s32[512]{0:T(512)S(1)}, s32[512]{0:T(512)}, u32[]{:S(2)}) copy-start(s32[512]{0:T(512)} %copy-done.29) | copy-start | bytes 6148
  351.2 85.8 %copy-start.28 = (s32[512]{0:T(512)S(1)}, s32[512]{0:T(512)}, u32[]{:S(2)}) copy-start(s32[512]{0:T(512)} %copy-done.27) | copy-start | bytes 6148
  436.9 38.6 %copy-start.26 = (s32[512]{0:T(512)S(1)}, s32[512]{0:T(512)}, u32[]{:S(2)}) copy-start(s32[512]{0:T(512)} %copy-done.25) | copy-start | bytes 6148
  475.6 15.4 %copy-start.10 = (f32[16,32]{0,1:T(8,128)S(1)}, f32[16,32]{0,1:T(8,128)}, u32[]{:S(2)}) copy-start(f32[16,32]{0,1:T(8,128)} %copy-done.9) | copy-start | bytes 6148
  475.6 15.3 %copy-start.13 = (f32[16,32]{0,1:T(8,128)S(1)}, f32[16,32]{0,1:T(8,128)}, u32[]{:S(2)}) copy-start(f32[16,32]{0,1:T(8,128)} %copy.121) | copy-start | bytes 6148
  475.6 15.3 %copy-start.14 = (f32[16,32]{0,1:T(8,128)S(1)}, f32[16,32]{0,1:T(8,128)}, u32[]{:S(2)}) copy-start(f32[16,32]{0,1:T(8,128)} %copy.119) | copy-start | bytes 6148
  475.6 15.3 %copy-start.15 = (f32[16,32]{0,1:T(8,128)S(1)}, f32[16,32]{0,1:T(8,128)}, u32[]{:S(2)}) copy-start(f32[16,32]{0,1:T(8,128)} %copy.117) | copy-start | bytes 6148
  475.6 15.3 %copy-start.16 = (f32[16,32]{0,1:T(8,128)S(1)}, f32[16,32]{0,1:T(8,128)}, u32[]{:S(2)}) copy-start(f32[16,32]{0,1:T(8,128)} %copy.115) | copy-start | bytes 6148
  475.6 15.3 %copy-start.17 = (f32[16,32]{0,1:T(8,128)S(1)}, f32[16,32]{0,1:T(8,128)}, u32[]{:S(2)}) copy-start(f32[16,32]{0,1:T(8,128)} %copy.113) | copy-start | bytes 6148
  475.7 15.3 %copy-start.18 = (f32[16,32]{0,1:T(8,128)S(1)}, f32[16,32]{0,1:T(8,128)}, u32[]{:S(2)}) copy-start(f32[16,32]{0,1:T(8,128)} %copy.111) | copy-start | bytes 6148
  475.7 15.3 %copy-start.19 = (f32[16,32]{0,1:T(8,128)S(1)}, f32[16,32]{0,1:T(8,128)}, u32[]{:S(2)}) copy-start(f32[16,32]{0,1:T(8,128)} %copy.109) | copy-start | bytes 6148
  (6 other events, 7.5 us)
where the time goes:
time: 513 us; the launch traced here: 511 us
  waiting for transfers between devices  278 us (54%)
  starting transfers between devices  92 us (18%)
  local copies, waits for them, and re-layouts  74.3 us (14%)
  matrix products  25 us (5%)
  between operations  14.6 us (3%)
  blocking collectives  13.6 us (3%)
  other arithmetic  13 us (3%)
    ppermute x9, waiting for transfers between devices, shifted_2(): return lax.ppermute(block, axis, route)  273 us
    ppermute x9, starting transfers between devices, shifted_2(): return lax.ppermute(block, axis, route)  85.7 us
    unnamed x94, local copies, waits for them, and re-layouts  38.6 us
    dot_general x14, matrix products, contract(): jnp.einsum(pattern, left_side, right_side, precision=lax.Precision.HIGHEST)  25 us
    all_to_all x1, blocking collectives, local(): lax.all_to_all(payload, 'fsdp', split_axis=0, concat_axis=1, tiled=True)  13.6 us
    all_to_all x1, local copies, waits for them, and re-layouts, local(): lax.all_to_all(streams, 'fsdp', split_axis=2, concat_axis=1, tiled=True)  11.8 us
  transfers between devices with their start and end apart: 10, of which 7 were waited for; matrix products, arithmetic and copies ran while one was open for 9% of the time, Pallas kernels for 0%

commit v1 on v0

v1 whole, which is shorter than its diff:
```python
import functools

import jax
import jax.numpy as jnp
from jax import lax
from jax.experimental import pallas as pl
from jax.experimental.pallas import tpu as pltpu
from jax.sharding import PartitionSpec as P

MESH = pl.DeviceIdType.MESH
GROUP = 16
MODES = 16
DOC_MAX = 4096
LANES = 128
BLOCK = 128
PACK = LANES // GROUP
F32 = jnp.float32
BF16 = jnp.bfloat16


def iota(shape, dim):
    return lax.broadcasted_iota(jnp.int32, shape, dim)


def halves(value):
    high = value.astype(BF16)
    return high, (value - high.astype(F32)).astype(BF16)


def one_minus_exp_neg(y):
    total = jnp.ones_like(y)
    for order in range(10, 1, -1):
        total = 1.0 - total * y * (1.0 / order)
    return total * y


def fused(
    n_ctx, n_fsdp, rows, look,
    streams, halo, segs, taps, decay, residue, skip, out,
    x, hb, hf, sg, tp, dc, rs, sk, marks, gs, v, qs, ms, mr, inner, fresh, kc, cl, ri, dcy, es, er,
    in_sem, tap_send, tap_recv, halo_send, halo_recv, g_send, g_recv, e_send, e_recv, m_send, m_recv,
):
    ctx, f = lax.axis_index("ctx"), lax.axis_index("fsdp")
    supers, members = n_ctx // 2, 2 * n_fsdp
    tile, half = ctx // 2, lax.rem(ctx, 2)
    r = half * n_fsdp + f
    per = members * rows
    blocks = per // BLOCK
    in_block = BLOCK // rows
    width = v.shape[2]
    lane_tiles = width // LANES
    chunks = x.shape[2] // LANES

    def member(p):
        return (2 * tile + p // n_fsdp, lax.rem(p, n_fsdp))

    def at_super(step):
        return (2 * lax.rem(tile + step, supers) + half, f)

    def tap_copy(owner, to):
        return pltpu.make_async_remote_copy(
            src_ref=tp.at[owner], dst_ref=tp.at[owner], send_sem=tap_send.at[to],
            recv_sem=tap_recv.at[owner], device_id=(ctx, to), device_id_type=MESH,
        )

    first = (r == 0).astype(jnp.int32)
    last = (r == members - 1).astype(jnp.int32)
    after = (
        jnp.where(r == members - 1, 2 * lax.rem(tile + 1, supers), 2 * tile + (r + 1) // n_fsdp),
        lax.rem(f + 1, n_fsdp),
    )

    def halo_copy():
        return pltpu.make_async_remote_copy(
            src_ref=halo, dst_ref=hb, send_sem=halo_send, recv_sem=halo_recv,
            device_id=after, device_id_type=MESH,
        )

    def block_copy(src, dst, sends, recvs, to, slot):
        return pltpu.make_async_remote_copy(
            src_ref=src.at[to], dst_ref=dst.at[slot], send_sem=sends.at[to],
            recv_sem=recvs.at[slot], device_id=member(to), device_id_type=MESH,
        )

    def state_copy(d):
        return pltpu.make_async_remote_copy(
            src_ref=es, dst_ref=er.at[d - 1], send_sem=e_send.at[d - 1],
            recv_sem=e_recv.at[d - 1], device_id=at_super(d), device_id_type=MESH,
        )

    loads = [
        pltpu.make_async_copy(decay, dc, in_sem.at[0]),
        pltpu.make_async_copy(residue, rs, in_sem.at[1]),
        pltpu.make_async_copy(skip, sk, in_sem.at[2]),
        pltpu.make_async_copy(segs, sg, in_sem.at[3]),
        pltpu.make_async_copy(taps, tp.at[f], in_sem.at[4]),
        pltpu.make_async_copy(streams, x, in_sem.at[5]),
    ]
    for load in loads:
        load.start()

    barrier = pltpu.get_barrier_semaphore()

    @pl.loop(1, members)
    def _(k):
        pl.semaphore_signal(
            barrier, inc=1, device_id=member(lax.rem(r + k, members)), device_id_type=MESH
        )

    for d in range(1, look + 1):
        pl.semaphore_signal(barrier, inc=1, device_id=at_super(supers - d), device_id_type=MESH)

    @pl.when(r == 0)
    def _():
        pl.semaphore_signal(
            barrier, inc=1, device_id=(2 * lax.rem(tile + supers - 1, supers) + 1, n_fsdp - 1),
            device_id_type=MESH,
        )

    for load in loads[:4]:
        load.wait()
    square = (BLOCK, BLOCK)
    down, across = iota(square, 0), iota(square, 1)
    eye = down == across
    causal = down >= across
    same_group = (down // MODES) == (across // GROUP)
    away = lax.rem(BLOCK - across, BLOCK).astype(F32)

    def to_column(row):
        return jnp.sum(jnp.where(eye, jnp.broadcast_to(row, square), 0.0), axis=1, keepdims=True)

    def mark_row(index):
        return sg[pl.ds(index, 1), :].astype(F32)

    for m in range(lane_tiles):
        base = half * (lane_tiles * PACK) + m * PACK
        rates = dc[pl.ds(base, PACK), :]
        gains = rs[pl.ds(base, PACK), :] * jnp.sqrt(one_minus_exp_neg(2.0 * rates))

        def spread(small):
            tall = jnp.broadcast_to(small[:, None, :], (PACK, MODES, MODES)).reshape(BLOCK, MODES)
            own = lax.rem(iota((BLOCK, MODES), 0), MODES) == iota((BLOCK, MODES), 1)
            return jnp.sum(jnp.where(own, tall, 0.0), axis=1, keepdims=True)

        rate = jnp.broadcast_to(spread(rates), square)
        gain = jnp.broadcast_to(spread(gains), square)
        rate_row = jnp.sum(jnp.where(eye, rate, 0.0), axis=0, keepdims=True)
        gain_row = jnp.sum(jnp.where(eye, gain, 0.0), axis=0, keepdims=True)
        dcy[m] = rate
        rise = gain_row * jnp.exp(-rate_row * (down + 1).astype(F32))
        high, low = halves(rise)
        ri[m] = jnp.concatenate([high, low, high], axis=1)
        close = jnp.exp(-rate * (BLOCK - 1 - across).astype(F32))
        high, low = halves(close)
        cl[m] = jnp.concatenate([high, low], axis=1)
        taps_of = jnp.sum(
            (gain * jnp.exp(-rate * away)).reshape(PACK, MODES, BLOCK), axis=1
        )
        for g in range(PACK):
            line = jnp.broadcast_to(taps_of[g : g + 1, :], square)
            line = pltpu.roll(line, 0, 1, stride=1, stride_axis=0)
            kc[m, :, g * BLOCK : (g + 1) * BLOCK] = jnp.where(causal, line, 0.0).astype(BF16)

    top = tile * blocks
    before_row = mark_row(jnp.maximum(top - 1, 0))
    before_col = to_column(before_row)[BLOCK - 8 :]
    before_col = jnp.where(tile > 0, before_col, -1.0)
    marks[0:8, :] = jnp.broadcast_to(before_col, (8, LANES))
    for b in range(blocks):
        marks[8 + b * BLOCK : 8 + (b + 1) * BLOCK, :] = jnp.broadcast_to(
            to_column(mark_row(top + b)), square
        )

    loads[4].wait()
    pl.semaphore_wait(barrier, members - 1 + look + last)

    halo_copy().start()

    @pl.loop(1, n_fsdp)
    def _(k):
        tap_copy(f, lax.rem(f + k, n_fsdp)).start()

    loads[5].wait()
    halo_copy().wait_recv()
    hf[...] = hb[...].astype(F32)

    window = marks[pl.ds(pl.multiple_of(r * rows, rows), rows + 8), :]
    own_marks = window[8:]
    agree = [None] + [window[8 - j : 8 - j + rows] == own_marks for j in (1, 2)]
    row_id = iota((rows, LANES), 0)

    def feature(s, owner, lane, chunk):
        col = pl.ds(pl.multiple_of(chunk * LANES, LANES), LANES)
        now = x[s, :, col].astype(F32)
        prev1 = hf[2 * s + 1, pl.ds(chunk, 1), :]
        prev2 = hf[2 * s, pl.ds(chunk, 1), :]
        shift1 = jnp.where(row_id == 0, prev1, pltpu.roll(now, 1, 0))
        shift2 = jnp.where(row_id == 0, prev2, jnp.where(row_id == 1, prev1, pltpu.roll(now, 2, 0)))

        def tap(j):
            return tp[owner, s, pl.ds(j, 1), lane * LANES : (lane + 1) * LANES]

        total = now * tap(0)
        total = total + jnp.where(agree[1], shift1, 0.0) * tap(1)
        return total + jnp.where(agree[2], shift2, 0.0) * tap(2)

    @pl.loop(0, n_fsdp)
    def _(k):
        owner = lax.rem(f + k, n_fsdp)

        @pl.when(k > 0)
        def _():
            tap_copy(owner, f).wait_recv()

        for part in range(2):
            to = part * n_fsdp + owner
            for m in range(lane_tiles):
                lane = part * lane_tiles + m
                chunk = owner * (2 * lane_tiles) + lane
                col = pl.ds(pl.multiple_of(chunk * LANES, LANES), LANES)
                qs[:, col] = feature(0, owner, lane, chunk).astype(BF16)
                gated = feature(1, owner, lane, chunk) * feature(2, owner, lane, chunk)
                gs[to, :, m * LANES : (m + 1) * LANES] = gated.astype(BF16)

            @pl.when(to != r)
            def _():
                block_copy(gs, v, g_send, g_recv, to, r).start()

    v[r] = gs[r]

    def marks_of(b):
        return marks[8 + b * BLOCK : 8 + (b + 1) * BLOCK, :]

    def end_mark(b):
        if b < 0:
            return marks[7:8, :]
        return marks[7 + (b + 1) * BLOCK : 8 + (b + 1) * BLOCK, :]

    def values(b, m):
        four = v[b * in_block : (b + 1) * in_block, :, m * LANES : (m + 1) * LANES]
        return four.reshape(BLOCK, LANES)

    spot = same_group.astype(F32)
    for b in range(blocks):
        for p in range(b * in_block, (b + 1) * in_block):

            @pl.when(r != p)
            def _(p=p):
                block_copy(gs, v, g_send, g_recv, r, p).wait_recv()

        ending = (marks_of(b) == end_mark(b)).astype(F32)
        for m in range(lane_tiles):
            kept = (values(b, m).astype(F32) * ending).astype(BF16)
            fresh[b, m] = spot * jnp.dot(
                cl[m], jnp.concatenate([kept, kept], axis=0), preferred_element_type=F32
            )

    for m in range(lane_tiles):
        fade = jnp.exp(-dcy[m] * float(BLOCK))
        state = fresh[0, m]
        for b in range(1, blocks):
            passing = (end_mark(b) == end_mark(b - 1)).astype(F32)
            state = passing * fade * state + fresh[b, m]
        es[:, m * LANES : (m + 1) * LANES] = jnp.sum(
            state.reshape(PACK, MODES, LANES), axis=0
        )
    for d in range(look, 0, -1):
        state_copy(d).start()

    lane_group = iota((1, LANES), 1) // GROUP
    for b in range(blocks):
        row = jnp.broadcast_to(mark_row(top + b), square)
        agreeing = (marks_of(b) == row).astype(BF16)
        agreeing = jnp.concatenate([agreeing] * PACK, axis=1)
        for m in range(lane_tiles):
            vals = values(b, m)
            parts = [vals * (lane_group == g).astype(BF16) for g in range(PACK)]
            direct = jnp.dot(
                kc[m] * agreeing, jnp.concatenate(parts, axis=0), preferred_element_type=F32
            )
            gain = sk[pl.ds(half * lane_tiles + m, 1), :]
            inner[b, m] = direct + gain * vals.astype(F32)

    first_mark = marks[8:9, :]
    for d in range(1, look + 1):
        state_copy(d).wait_recv()
    states = []
    for m in range(lane_tiles):
        state = jnp.zeros(square, F32)
        for d in range(1, look + 1):
            source = lax.rem(tile + supers - d, supers)
            its_end = mark_row(source * blocks + blocks - 1)[:, LANES - 1 :]
            joined = (jnp.broadcast_to(its_end, (1, LANES)) == first_mark).astype(F32)
            joined = jnp.where(tile >= d, joined, 0.0)
            part = er[d - 1, :, m * LANES : (m + 1) * LANES]
            part = jnp.concatenate([part] * PACK, axis=0)
            if d > 1:
                part = part * jnp.exp(-dcy[m] * float(per * (d - 1)))
            state = state + joined * part
        states.append(spot * state)

    for b in range(blocks):
        follow = (marks_of(b) == end_mark(b - 1)).astype(F32)
        passing = (end_mark(b) == end_mark(b - 1)).astype(F32)
        for m in range(lane_tiles):
            high, low = halves(states[m])
            brought = jnp.dot(
                ri[m], jnp.concatenate([high, high, low], axis=0), preferred_element_type=F32
            )
            mixed = (inner[b, m] + follow * brought).astype(BF16)
            ms[b * in_block : (b + 1) * in_block, :, m * LANES : (m + 1) * LANES] = mixed.reshape(
                in_block, rows, LANES
            )
            if b < blocks - 1:
                fade = jnp.exp(-dcy[m] * float(BLOCK))
                states[m] = passing * fade * states[m] + fresh[b, m]
        for p in range(b * in_block, (b + 1) * in_block):

            @pl.when(r != p)
            def _(p=p):
                block_copy(ms, mr, m_send, m_recv, p, r).start()

    mr[r] = ms[r]

    @pl.loop(0, members)
    def _(k):
        source = lax.rem(r + k, members)

        @pl.when(k > 0)
        def _():
            block_copy(ms, mr, m_send, m_recv, r, source).wait_recv()

        base = lax.rem(source, n_fsdp) * (2 * width) + (source // n_fsdp) * width
        col = pl.ds(pl.multiple_of(base, width), width)
        out[:, col] = (qs[:, col].astype(F32) * mr[source].astype(F32)).astype(BF16)

    halo_copy().wait_send()

    @pl.loop(1, n_fsdp)
    def _(k):
        tap_copy(f, lax.rem(f + k, n_fsdp)).wait_send()

    @pl.loop(1, members)
    def _(k):
        to = lax.rem(r + k, members)
        block_copy(gs, v, g_send, g_recv, to, r).wait_send()
        block_copy(ms, mr, m_send, m_recv, to, r).wait_send()

    for d in range(1, look + 1):
        state_copy(d).wait_send()


def local(streams, segments, short_taps, decay_rates, residues, skip_gain):
    n_ctx, n_fsdp = lax.axis_size("ctx"), lax.axis_size("fsdp")
    rows, model = streams.shape[1:]
    supers, members = n_ctx // 2, 2 * n_fsdp
    width = model // members
    lane_tiles = width // LANES
    per = members * rows
    blocks = per // BLOCK
    look = min(-(-DOC_MAX // per), supers - 1)
    groups = width // GROUP
    halo = streams[:, rows - 2 :, :].reshape(6, model // LANES, LANES)
    segs = segments.reshape(-1, LANES)
    skip = skip_gain.reshape(-1, LANES)
    any_space = pl.BlockSpec(memory_space=pl.ANY)
    dma = pltpu.SemaphoreType.DMA
    square = (BLOCK, BLOCK)
    vmem = pltpu.VMEM
    return pl.pallas_call(
        functools.partial(fused, n_ctx, n_fsdp, rows, look),
        out_shape=jax.ShapeDtypeStruct((rows, model), BF16),
        in_specs=[any_space] * 7,
        out_specs=pl.BlockSpec(memory_space=vmem),
        scratch_shapes=[
            vmem((3, rows, model), BF16),
            vmem((6, model // LANES, LANES), BF16),
            vmem((6, model // LANES, LANES), F32),
            vmem(segs.shape, jnp.int32),
            vmem((n_fsdp, *short_taps.shape), F32),
            vmem(decay_rates.shape, F32),
            vmem(residues.shape, F32),
            vmem(skip.shape, F32),
            vmem((8 + per, LANES), F32),
            vmem((members, rows, width), BF16),
            vmem((members, rows, width), BF16),
            vmem((rows, model), BF16),
            vmem((members, rows, width), BF16),
            vmem((members, rows, width), BF16),
            vmem((blocks, lane_tiles, *square), F32),
            vmem((blocks, lane_tiles, *square), F32),
            vmem((lane_tiles, BLOCK, PACK * BLOCK), BF16),
            vmem((lane_tiles, BLOCK, 2 * BLOCK), BF16),
            vmem((lane_tiles, BLOCK, 3 * BLOCK), BF16),
            vmem((lane_tiles, *square), F32),
            vmem((MODES, width), F32),
            vmem((look, MODES, width), F32),
            dma((6,)),
            dma((n_fsdp,)),
            dma((n_fsdp,)),
            dma(()),
            dma(()),
            dma((members,)),
            dma((members,)),
            dma((look,)),
            dma((look,)),
            dma((members,)),
            dma((members,)),
        ],
        compiler_params=pltpu.CompilerParams(
            collective_id=0, has_side_effects=True, vmem_limit_bytes=48 << 20
        ),
    )(streams, halo, segs, short_taps, decay_rates, residues, skip)


def solution(mesh):
    placed = (
        P(None, ("ctx", "fsdp"), None),
        P(),
        P(None, None, "fsdp"),
        P("fsdp", None),
        P("fsdp", None),
        P("fsdp"),
    )
    return jax.shard_map(
        local, mesh=mesh, in_specs=placed, out_specs=P(("ctx", "fsdp"), None), check_vma=False
    )
```

time: 513 us -> 60.7 us (0.12)
  the two profiles are of different devices: /device:TPU:7 before, /device:TPU:29 now
where the time goes in v1:
time: 60.7 us; the launch traced here: 60.3 us
  Pallas kernels  53.1 us (87%)
  local copies, waits for them, and re-layouts  7.18 us (12%)
    pallas_call x1, Pallas kernels, local(): pl.pallas_call(functools.partial(fused, n_ctx, n_fsdp, rows, look), out_s...  53.1 us
    unnamed x11, local copies, waits for them, and re-layouts  6 us

profile of v1, /device:TPU:29, one launch (start us, length us, event | category | flops | bytes accessed | tf_op | source)
XLA Modules:
  0.0 60.3 jit_solution(9250644239279620351)
XLA Ops:
  0.0 0.8 %copy.9.decay = f32[32,16]{1,0:T(8,128)S(1)} copy(f32[32,16]{0,1:T(8,128)} %param.9) | data formatting | bytes 4096 | tf_op args[3]
  0.8 0.8 %copy.10.residue = f32[32,16]{1,0:T(8,128)S(1)} copy(f32[32,16]{0,1:T(8,128)} %param.10) | data formatting | bytes 4096 | tf_op args[4]
  1.5 1.1 %slice.3 = bf16[3,2,8192]{2,1,0:T(2,128)(2,1)S(1)} slice(bf16[3,32,8192]{2,1,0:T(8,128)(2,1)} %streams.1), slice={[0:3], [30:32], [0:8192]} | slice | bytes 196608 | tf_op jit(solution)/shard_map/slice | solution.py:363
  2.6 0.1 reshape.9.halo
  2.7 0.0 copy-start
  2.7 1.4 %copy-done = bf16[3,32,8192]{2,1,0:T(8,128)(2,1)S(1)} copy-done((bf16[3,32,8192]{2,1,0:T(8,128)(2,1)S(1)}, bf16[3,32,8192]{2,1,0:T(8,128)(2,1)}, u32[]{:S(2)}) %copy-start) | copy-done | bytes 1572888
  4.1 0.0 copy-start.1
  4.1 0.8 %copy-done.1 = s32[16384]{0:T(1024)S(1)} copy-done((s32[16384]{0:T(1024)S(1)}, s32[16384]{0:T(1024)}, u32[]{:S(2)}) %copy-start.1) | copy-done | bytes 65560
  5.0 0.0 copy-start.2
  5.0 0.7 %copy-done.2 = f32[3,3,512]{2,1,0:T(4,128)S(1)} copy-done((f32[3,3,512]{2,1,0:T(4,128)S(1)}, f32[3,3,512]{2,1,0:T(4,128)}, u32[]{:S(2)}) %copy-start.2) | copy-done | bytes 18456
  5.7 0.0 copy-start.3
  5.7 0.7 %copy-done.3 = f32[512]{0:T(512)S(1)} copy-done((f32[512]{0:T(512)S(1)}, f32[512]{0:T(512)}, u32[]{:S(2)}) %copy-start.3) | copy-done | bytes 2072
  6.4 53.1 %shard_map.64 = bf16[32,8192]{1,0:T(8,128)(2,1)S(1)} custom-call(bf16[3,32,8192]{2,1,0:T(8,128)(2,1)S(1)} %copy-done, bf16[6,64,128]{2,1,0:T(8,128)(2,1)S(1)} %reshape.9.halo, s32[128,128]{1,0:T(8,128)S(1)} %bitcast.2, f32[3,3,512]{2,1,0:T(4,128)S(1)} %copy-done.2, f32[32,16]{1,0:T(8,128)S(1)} %copy.9.decay, f32[32,16]{1,0:T(8,128)S(1)} %copy.10.residue, ...), custom_call_target="tpu_custom_call" | custom-call | tf_op jit(solution)/shard_map/pallas_call | solution.py:370
  59.5 0.8 %copy.12 = bf16[32,8192]{1,0:T(8,128)(2,1)} copy(bf16[32,8192]{1,0:T(8,128)(2,1)S(1)} %shard_map.64) | data formatting | bytes 1048576
Async XLA Ops:
  2.7 1.4 %copy-start = (bf16[3,32,8192]{2,1,0:T(8,128)(2,1)S(1)}, bf16[3,32,8192]{2,1,0:T(8,128)(2,1)}, u32[]{:S(2)}) copy-start(bf16[3,32,8192]{2,1,0:T(8,128)(2,1)} %streams.1) | copy-start | bytes 4718596
  4.1 0.8 %copy-start.1 = (s32[16384]{0:T(1024)S(1)}, s32[16384]{0:T(1024)}, u32[]{:S(2)}) copy-start(s32[16384]{0:T(1024)} %param.7) | copy-start | bytes 196612
  5.0 0.7 %copy-start.2 = (f32[3,3,512]{2,1,0:T(4,128)S(1)}, f32[3,3,512]{2,1,0:T(4,128)}, u32[]{:S(2)}) copy-start(f32[3,3,512]{2,1,0:T(4,128)} %taps.1) | copy-start | bytes 55300
  5.7 0.7 %copy-start.3 = (f32[512]{0:T(512)S(1)}, f32[512]{0:T(512)}, u32[]{:S(2)}) copy-start(f32[512]{0:T(512)} %param.11) | copy-start | bytes 6148

commit v2 on v1

--- a/solution.py
+++ b/solution.py
@@ -36,9 +36,9 @@
 
 def fused(
     n_ctx, n_fsdp, rows, look,
-    streams, halo, segs, taps, decay, residue, skip, out,
-    x, hb, hf, sg, tp, dc, rs, sk, marks, gs, v, qs, ms, mr, inner, fresh, kc, cl, ri, dcy, es, er,
-    in_sem, tap_send, tap_recv, halo_send, halo_recv, g_send, g_recv, e_send, e_recv, m_send, m_recv,
+    streams, segs, taps, decay, residue, skip, out,
+    x, hs, hb, hf, sg, own_taps, tp, dc, rs, sk, marks, gs, v, qs, ms, mr, inner, fresh, kc, cl, ri, dcy, carry, es, er,
+    in_sem, tap_send, tap_recv, halo_send, halo_recv, g_send, g_recv, e_send, e_recv, m_send, m_recv, hello, ready,
 ):
     ctx, f = lax.axis_index("ctx"), lax.axis_index("fsdp")
     supers, members = n_ctx // 2, 2 * n_fsdp
@@ -49,13 +49,13 @@
     in_block = BLOCK // rows
     width = v.shape[2]
     lane_tiles = width // LANES
-    chunks = x.shape[2] // LANES
+    quads = own_taps.shape[2] // LANES
 
     def member(p):
         return (2 * tile + p // n_fsdp, lax.rem(p, n_fsdp))
 
     def at_super(step):
-        return (2 * lax.rem(tile + step, supers) + half, f)
+        return (ctx + 2 * step, f)
 
     def tap_copy(owner, to):
         return pltpu.make_async_remote_copy(
@@ -63,17 +63,14 @@
             recv_sem=tap_recv.at[owner], device_id=(ctx, to), device_id_type=MESH,
         )
 
-    first = (r == 0).astype(jnp.int32)
-    last = (r == members - 1).astype(jnp.int32)
-    after = (
-        jnp.where(r == members - 1, 2 * lax.rem(tile + 1, supers), 2 * tile + (r + 1) // n_fsdp),
-        lax.rem(f + 1, n_fsdp),
-    )
+    more = tile < supers - 1
+    sends_halo = more | (r < members - 1)
+    gets_halo = (tile > 0) | (r > 0)
 
     def halo_copy():
         return pltpu.make_async_remote_copy(
-            src_ref=halo, dst_ref=hb, send_sem=halo_send, recv_sem=halo_recv,
-            device_id=after, device_id_type=MESH,
+            src_ref=hs, dst_ref=hb, send_sem=halo_send, recv_sem=halo_recv,
+            device_id=(2 * tile + (r + 1) // n_fsdp, lax.rem(f + 1, n_fsdp)), device_id_type=MESH,
         )
 
     def block_copy(src, dst, sends, recvs, to, slot):
@@ -81,6 +78,30 @@
             src_ref=src.at[to], dst_ref=dst.at[slot], send_sem=sends.at[to],
             recv_sem=recvs.at[slot], device_id=member(to), device_id_type=MESH,
         )
+
+    def pass_ready(hop):
+        if hop > look:
+            return
+        known = tile + hop < supers
+        if hop == 1:
+
+            @pl.when(tile > 0)
+            def _():
+                pl.semaphore_wait(hello, 1)
+
+        else:
+
+            @pl.when(known)
+            def _():
+                pl.semaphore_wait(ready.at[hop - 2], 1)
+
+        if hop < look:
+
+            @pl.when(known & (tile > 0))
+            def _():
+                pl.semaphore_signal(
+                    ready.at[hop - 1], inc=1, device_id=at_super(-1), device_id_type=MESH
+                )
 
     def state_copy(d):
         return pltpu.make_async_remote_copy(
@@ -93,7 +114,7 @@
         pltpu.make_async_copy(residue, rs, in_sem.at[1]),
         pltpu.make_async_copy(skip, sk, in_sem.at[2]),
         pltpu.make_async_copy(segs, sg, in_sem.at[3]),
-        pltpu.make_async_copy(taps, tp.at[f], in_sem.at[4]),
+        pltpu.make_async_copy(taps, own_taps, in_sem.at[4]),
         pltpu.make_async_copy(streams, x, in_sem.at[5]),
     ]
     for load in loads:
@@ -107,14 +128,14 @@
             barrier, inc=1, device_id=member(lax.rem(r + k, members)), device_id_type=MESH
         )
 
-    for d in range(1, look + 1):
-        pl.semaphore_signal(barrier, inc=1, device_id=at_super(supers - d), device_id_type=MESH)
-
-    @pl.when(r == 0)
+    @pl.when(tile > 0)
+    def _():
+        pl.semaphore_signal(barrier, inc=1, device_id=at_super(-1), device_id_type=MESH)
+
+    @pl.when((tile > 0) & (r == 0))
     def _():
         pl.semaphore_signal(
-            barrier, inc=1, device_id=(2 * lax.rem(tile + supers - 1, supers) + 1, n_fsdp - 1),
-            device_id_type=MESH,
+            barrier, inc=1, device_id=(2 * tile - 1, n_fsdp - 1), device_id_type=MESH
         )
 
     for load in loads[:4]:
@@ -132,14 +153,14 @@
     def mark_row(index):
         return sg[pl.ds(index, 1), :].astype(F32)
 
+    rates = dc[...]
+    gains = rs[...] * jnp.sqrt(one_minus_exp_neg(2.0 * rates))
     for m in range(lane_tiles):
         base = half * (lane_tiles * PACK) + m * PACK
-        rates = dc[pl.ds(base, PACK), :]
-        gains = rs[pl.ds(base, PACK), :] * jnp.sqrt(one_minus_exp_neg(2.0 * rates))
+        own = iota((BLOCK, rates.shape[1]), 1) == base + iota((BLOCK, rates.shape[1]), 0) // MODES
 
         def spread(small):
-            tall = jnp.broadcast_to(small[:, None, :], (PACK, MODES, MODES)).reshape(BLOCK, MODES)
-            own = lax.rem(iota((BLOCK, MODES), 0), MODES) == iota((BLOCK, MODES), 1)
+            tall = jnp.concatenate([small] * PACK, axis=0)
             return jnp.sum(jnp.where(own, tall, 0.0), axis=1, keepdims=True)
 
         rate = jnp.broadcast_to(spread(rates), square)
@@ -172,17 +193,50 @@
         )
 
     loads[4].wait()
-    pl.semaphore_wait(barrier, members - 1 + look + last)
-
-    halo_copy().start()
+    for s in range(3):
+        for j in range(3):
+            for q in range(quads):
+                row = (s * 3 + j) * quads + q
+                tp[f, row : row + 1, :] = own_taps[s, j : j + 1, q * LANES : (q + 1) * LANES]
+
+    loads[5].wait()
+    step = 4 * LANES
+    slot = iota((8, step), 0) // 2
+
+    @pl.loop(0, x.shape[2] // step)
+    def _(k):
+        col = pl.ds(pl.multiple_of(k * step, step), step)
+        total = jnp.zeros((8, step), F32)
+        for s in range(3):
+            tail = x[s, rows - 8 : rows, col].astype(F32)
+            total = jnp.where(slot == s, pltpu.roll(tail, 2 * s + 2, 0), total)
+        hs[:, col] = total.astype(BF16)
+
+    greets = jnp.where(more, 1, 0) + jnp.where(more & (r == members - 1), 1, 0)
+    pl.semaphore_wait(barrier, members - 1 + greets)
+
+    @pl.when(sends_halo)
+    def _():
+        halo_copy().start()
 
     @pl.loop(1, n_fsdp)
     def _(k):
         tap_copy(f, lax.rem(f + k, n_fsdp)).start()
 
-    loads[5].wait()
-    halo_copy().wait_recv()
-    hf[...] = hb[...].astype(F32)
+    @pl.when(more)
+    def _():
+        pl.semaphore_signal(hello, inc=1, device_id=at_super(1), device_id_type=MESH)
+
+    @pl.when(gets_halo)
+    def _():
+        halo_copy().wait_recv()
+        hf[...] = hb[...].astype(F32)
+
+    @pl.when(jnp.logical_not(gets_halo))
+    def _():
+        hf[...] = jnp.zeros_like(hf)
+
+    pass_ready(1)
 
     window = marks[pl.ds(pl.multiple_of(r * rows, rows), rows + 8), :]
     own_marks = window[8:]
@@ -192,13 +246,14 @@
     def feature(s, owner, lane, chunk):
         col = pl.ds(pl.multiple_of(chunk * LANES, LANES), LANES)
         now = x[s, :, col].astype(F32)
-        prev1 = hf[2 * s + 1, pl.ds(chunk, 1), :]
-        prev2 = hf[2 * s, pl.ds(chunk, 1), :]
+        prev1 = hf[2 * s + 1 : 2 * s + 2, col]
+        prev2 = hf[2 * s : 2 * s + 1, col]
         shift1 = jnp.where(row_id == 0, prev1, pltpu.roll(now, 1, 0))
         shift2 = jnp.where(row_id == 0, prev2, jnp.where(row_id == 1, prev1, pltpu.roll(now, 2, 0)))
 
         def tap(j):
-            return tp[owner, s, pl.ds(j, 1), lane * LANES : (lane + 1) * LANES]
+            row = (s * 3 + j) * quads + lane
+            return tp[owner, row : row + 1, :]
 
         total = now * tap(0)
         total = total + jnp.where(agree[1], shift1, 0.0) * tap(1)
@@ -226,6 +281,7 @@
             def _():
                 block_copy(gs, v, g_send, g_recv, to, r).start()
 
+    pass_ready(2)
     v[r] = gs[r]
 
     def marks_of(b):
@@ -255,6 +311,7 @@
                 cl[m], jnp.concatenate([kept, kept], axis=0), preferred_element_type=F32
             )
 
+    pass_ready(3)
     for m in range(lane_tiles):
         fade = jnp.exp(-dcy[m] * float(BLOCK))
         state = fresh[0, m]
@@ -264,8 +321,14 @@
         es[:, m * LANES : (m + 1) * LANES] = jnp.sum(
             state.reshape(PACK, MODES, LANES), axis=0
         )
+    for hop in range(4, look + 1):
+        pass_ready(hop)
     for d in range(look, 0, -1):
-        state_copy(d).start()
+
+        @pl.when(tile + d < supers)
+        def _(d=d):
+            state_copy(d).start()
+
 
     lane_group = iota((1, LANES), 1) // GROUP
     for b in range(blocks):
@@ -282,22 +345,23 @@
             inner[b, m] = direct + gain * vals.astype(F32)
 
     first_mark = marks[8:9, :]
+    for m in range(lane_tiles):
+        carry[m] = jnp.zeros(square, F32)
     for d in range(1, look + 1):
-        state_copy(d).wait_recv()
-    states = []
-    for m in range(lane_tiles):
-        state = jnp.zeros(square, F32)
-        for d in range(1, look + 1):
-            source = lax.rem(tile + supers - d, supers)
-            its_end = mark_row(source * blocks + blocks - 1)[:, LANES - 1 :]
-            joined = (jnp.broadcast_to(its_end, (1, LANES)) == first_mark).astype(F32)
-            joined = jnp.where(tile >= d, joined, 0.0)
-            part = er[d - 1, :, m * LANES : (m + 1) * LANES]
-            part = jnp.concatenate([part] * PACK, axis=0)
-            if d > 1:
-                part = part * jnp.exp(-dcy[m] * float(per * (d - 1)))
-            state = state + joined * part
-        states.append(spot * state)
+
+        @pl.when(tile >= d)
+        def _(d=d):
+            state_copy(d).wait_recv()
+            its_end = mark_row((tile - d) * blocks + blocks - 1)[:, LANES - 1 :]
+            joined = spot * (jnp.broadcast_to(its_end, (1, LANES)) == first_mark).astype(F32)
+            for m in range(lane_tiles):
+                part = er[d - 1, :, m * LANES : (m + 1) * LANES]
+                part = joined * jnp.concatenate([part] * PACK, axis=0)
+                if d > 1:
+                    part = part * jnp.exp(-dcy[m] * float(per * (d - 1)))
+                carry[m] += part
+
+    states = [carry[m] for m in range(lane_tiles)]
 
     for b in range(blocks):
         follow = (marks_of(b) == end_mark(b - 1)).astype(F32)
@@ -334,7 +398,9 @@
         col = pl.ds(pl.multiple_of(base, width), width)
         out[:, col] = (qs[:, col].astype(F32) * mr[source].astype(F32)).astype(BF16)
 
-    halo_copy().wait_send()
+    @pl.when(sends_halo)
+    def _():
+        halo_copy().wait_send()
 
     @pl.loop(1, n_fsdp)
     def _(k):
@@ -347,7 +413,10 @@
         block_copy(ms, mr, m_send, m_recv, to, r).wait_send()
 
     for d in range(1, look + 1):
-        state_copy(d).wait_send()
+
+        @pl.when(tile + d < supers)
+        def _(d=d):
+            state_copy(d).wait_send()
 
 
 def local(streams, segments, short_taps, decay_rates, residues, skip_gain):
@@ -360,9 +429,9 @@
     blocks = per // BLOCK
     look = min(-(-DOC_MAX // per), supers - 1)
     groups = width // GROUP
-    halo = streams[:, rows - 2 :, :].reshape(6, model // LANES, LANES)
     segs = segments.reshape(-1, LANES)
     skip = skip_gain.reshape(-1, LANES)
+    rates, gains = decay_rates.T, residues.T
     any_space = pl.BlockSpec(memory_space=pl.ANY)
     dma = pltpu.SemaphoreType.DMA
     square = (BLOCK, BLOCK)
@@ -370,16 +439,18 @@
     return pl.pallas_call(
         functools.partial(fused, n_ctx, n_fsdp, rows, look),
         out_shape=jax.ShapeDtypeStruct((rows, model), BF16),
-        in_specs=[any_space] * 7,
+        in_specs=[any_space] * 6,
         out_specs=pl.BlockSpec(memory_space=vmem),
         scratch_shapes=[
             vmem((3, rows, model), BF16),
-            vmem((6, model // LANES, LANES), BF16),
-            vmem((6, model // LANES, LANES), F32),
+            vmem((8, model), BF16),
+            vmem((8, model), BF16),
+            vmem((8, model), F32),
             vmem(segs.shape, jnp.int32),
-            vmem((n_fsdp, *short_taps.shape), F32),
-            vmem(decay_rates.shape, F32),
-            vmem(residues.shape, F32),
+            vmem(short_taps.shape, F32),
+            vmem((n_fsdp, -(-9 * (short_taps.shape[2] // LANES) // 8) * 8, LANES), F32),
+            vmem(rates.shape, F32),
+            vmem(rates.shape, F32),
             vmem(skip.shape, F32),
             vmem((8 + per, LANES), F32),
             vmem((members, rows, width), BF16),
@@ -392,6 +463,7 @@
             vmem((lane_tiles, BLOCK, PACK * BLOCK), BF16),
             vmem((lane_tiles, BLOCK, 2 * BLOCK), BF16),
             vmem((lane_tiles, BLOCK, 3 * BLOCK), BF16),
+            vmem((lane_tiles, *square), F32),
             vmem((lane_tiles, *square), F32),
             vmem((MODES, width), F32),
             vmem((look, MODES, width), F32),
@@ -406,11 +478,13 @@
             dma((look,)),
             dma((members,)),
             dma((members,)),
+            pltpu.SemaphoreType.REGULAR,
+            pltpu.SemaphoreType.REGULAR((max(look - 1, 1),)),
         ],
         compiler_params=pltpu.CompilerParams(
-            collective_id=0, has_side_effects=True, vmem_limit_bytes=48 << 20
+            collective_id=0, has_side_effects=True, vmem_limit_bytes=60 * 1024 * 1024
         ),
-    )(streams, halo, segs, short_taps, decay_rates, residues, skip)
+    )(streams, segs, short_taps, rates, gains, skip)
 
 
 def solution(mesh):

time: 60.7 us -> 53.9 us (0.89)
  the two profiles are of different devices: /device:TPU:29 before, /device:TPU:61 now
where the time goes in v2:
time: 53.9 us; the launch traced here: 53.7 us
  Pallas kernels  51.8 us (96%)
  local copies, waits for them, and re-layouts  1.87 us (3%)
    pallas_call x1, Pallas kernels, local(): pl.pallas_call(functools.partial(fused, n_ctx, n_fsdp, rows, look), out_s...  51.8 us
    unnamed x1, local copies, waits for them, and re-layouts  1.87 us

profile of v2, /device:TPU:61, one launch (start us, length us, event | category | flops | bytes accessed | tf_op | source)
XLA Modules:
  0.0 53.7 jit_solution(4058760291184283717)
XLA Ops:
  0.0 51.8 %shard_map.64 = bf16[32,8192]{1,0:T(8,128)(2,1)} custom-call(bf16[3,32,8192]{2,1,0:T(8,128)(2,1)} %streams.1, s32[128,128]{1,0:T(8,128)} %bitcast.4, f32[3,3,512]{2,1,0:T(4,128)} %taps.1, f32[16,32]{1,0:T(8,128)} %bitcast.5, f32[16,32]{1,0:T(8,128)} %bitcast.6, f32[4,128]{1,0:T(4,128)} %bitcast.7), custom_call_target="tpu_custom_call" | custom-call | tf_op jit(solution)/shard_map/pallas_call | solution.py:439
  51.8 1.9 %copy.8 = bf16[32,8192]{1,0:T(8,128)(2,1)} copy(bf16[32,8192]{1,0:T(8,128)(2,1)} %shard_map.64) | data formatting | bytes 1048576

commit v3 on v2

--- a/solution.py
+++ b/solution.py
@@ -138,6 +138,41 @@
             barrier, inc=1, device_id=(2 * tile - 1, n_fsdp - 1), device_id_type=MESH
         )
 
+    loads[4].wait()
+    for s in range(3):
+        for j in range(3):
+            for q in range(quads):
+                row = (s * 3 + j) * quads + q
+                tp[f, row : row + 1, :] = own_taps[s, j : j + 1, q * LANES : (q + 1) * LANES]
+
+    greets = jnp.where(more, 1, 0) + jnp.where(more & (r == members - 1), 1, 0)
+    pl.semaphore_wait(barrier, members - 1 + greets)
+
+    @pl.loop(1, n_fsdp)
+    def _(k):
+        tap_copy(f, lax.rem(f + k, n_fsdp)).start()
+
+    loads[5].wait()
+    step = 4 * LANES
+    slot = iota((8, step), 0) // 2
+
+    @pl.loop(0, x.shape[2] // step)
+    def _(k):
+        col = pl.ds(pl.multiple_of(k * step, step), step)
+        total = jnp.zeros((8, step), F32)
+        for s in range(3):
+            tail = x[s, rows - 8 : rows, col].astype(F32)
+            total = jnp.where(slot == s, pltpu.roll(tail, 2 * s + 2, 0), total)
+        hs[:, col] = total.astype(BF16)
+
+    @pl.when(sends_halo)
+    def _():
+        halo_copy().start()
+
+    @pl.when(more)
+    def _():
+        pl.semaphore_signal(hello, inc=1, device_id=at_super(1), device_id_type=MESH)
+
     for load in loads[:4]:
         load.wait()
     square = (BLOCK, BLOCK)
@@ -192,41 +227,6 @@
             to_column(mark_row(top + b)), square
         )
 
-    loads[4].wait()
-    for s in range(3):
-        for j in range(3):
-            for q in range(quads):
-                row = (s * 3 + j) * quads + q
-                tp[f, row : row + 1, :] = own_taps[s, j : j + 1, q * LANES : (q + 1) * LANES]
-
-    loads[5].wait()
-    step = 4 * LANES
-    slot = iota((8, step), 0) // 2
-
-    @pl.loop(0, x.shape[2] // step)
-    def _(k):
-        col = pl.ds(pl.multiple_of(k * step, step), step)
-        total = jnp.zeros((8, step), F32)
-        for s in range(3):
-            tail = x[s, rows - 8 : rows, col].astype(F32)
-            total = jnp.where(slot == s, pltpu.roll(tail, 2 * s + 2, 0), total)
-        hs[:, col] = total.astype(BF16)
-
-    greets = jnp.where(more, 1, 0) + jnp.where(more & (r == members - 1), 1, 0)
-    pl.semaphore_wait(barrier, members - 1 + greets)
-
-    @pl.when(sends_halo)
-    def _():
-        halo_copy().start()
-
-    @pl.loop(1, n_fsdp)
-    def _(k):
-        tap_copy(f, lax.rem(f + k, n_fsdp)).start()
-
-    @pl.when(more)
-    def _():
-        pl.semaphore_signal(hello, inc=1, device_id=at_super(1), device_id_type=MESH)
-
     @pl.when(gets_halo)
     def _():
         halo_copy().wait_recv()
@@ -261,11 +261,17 @@
 
     @pl.loop(0, n_fsdp)
     def _(k):
-        owner = lax.rem(f + k, n_fsdp)
+        owner = lax.rem(f + n_fsdp - k, n_fsdp)
 
         @pl.when(k > 0)
         def _():
             tap_copy(owner, f).wait_recv()
+
+        for hop, point in ((2, n_fsdp // 4), (3, n_fsdp // 2)):
+
+            @pl.when(k == point)
+            def _(hop=hop):
+                pass_ready(hop)
 
         for part in range(2):
             to = part * n_fsdp + owner
@@ -281,7 +287,6 @@
             def _():
                 block_copy(gs, v, g_send, g_recv, to, r).start()
 
-    pass_ready(2)
     v[r] = gs[r]
 
     def marks_of(b):
@@ -311,7 +316,6 @@
                 cl[m], jnp.concatenate([kept, kept], axis=0), preferred_element_type=F32
             )
 
-    pass_ready(3)
     for m in range(lane_tiles):
         fade = jnp.exp(-dcy[m] * float(BLOCK))
         state = fresh[0, m]
@@ -320,10 +324,10 @@
             state = passing * fade * state + fresh[b, m]
         es[:, m * LANES : (m + 1) * LANES] = jnp.sum(
             state.reshape(PACK, MODES, LANES), axis=0
-        )
+        ).astype(BF16)
     for hop in range(4, look + 1):
         pass_ready(hop)
-    for d in range(look, 0, -1):
+    for d in range(1, look + 1):
 
         @pl.when(tile + d < supers)
         def _(d=d):
@@ -355,40 +359,48 @@
             its_end = mark_row((tile - d) * blocks + blocks - 1)[:, LANES - 1 :]
             joined = spot * (jnp.broadcast_to(its_end, (1, LANES)) == first_mark).astype(F32)
             for m in range(lane_tiles):
-                part = er[d - 1, :, m * LANES : (m + 1) * LANES]
+                part = er[d - 1, :, m * LANES : (m + 1) * LANES].astype(F32)
                 part = joined * jnp.concatenate([part] * PACK, axis=0)
                 if d > 1:
                     part = part * jnp.exp(-dcy[m] * float(per * (d - 1)))
                 carry[m] += part
 
-    states = [carry[m] for m in range(lane_tiles)]
-
-    for b in range(blocks):
-        follow = (marks_of(b) == end_mark(b - 1)).astype(F32)
-        passing = (end_mark(b) == end_mark(b - 1)).astype(F32)
+    for m in range(lane_tiles):
+        state = carry[m]
+        fade = jnp.exp(-dcy[m] * float(BLOCK))
+        for b in range(blocks):
+            kept = fresh[b, m]
+            fresh[b, m] = state
+            if b < blocks - 1:
+                passing = (end_mark(b) == end_mark(b - 1)).astype(F32)
+                state = passing * fade * state + kept
+
+    @pl.loop(0, blocks)
+    def _(k):
+        b = lax.rem(r // in_block + k, blocks)
+        start = pl.multiple_of(b * BLOCK, BLOCK)
+        follow = (marks[pl.ds(start + 8, BLOCK), :] == marks[pl.ds(start, 8), :][7:]).astype(F32)
         for m in range(lane_tiles):
-            high, low = halves(states[m])
+            high, low = halves(fresh[b, m])
             brought = jnp.dot(
                 ri[m], jnp.concatenate([high, high, low], axis=0), preferred_element_type=F32
             )
             mixed = (inner[b, m] + follow * brought).astype(BF16)
-            ms[b * in_block : (b + 1) * in_block, :, m * LANES : (m + 1) * LANES] = mixed.reshape(
+            ms[pl.ds(b * in_block, in_block), :, m * LANES : (m + 1) * LANES] = mixed.reshape(
                 in_block, rows, LANES
             )
-            if b < blocks - 1:
-                fade = jnp.exp(-dcy[m] * float(BLOCK))
-                states[m] = passing * fade * states[m] + fresh[b, m]
-        for p in range(b * in_block, (b + 1) * in_block):
-
-            @pl.when(r != p)
-            def _(p=p):
-                block_copy(ms, mr, m_send, m_recv, p, r).start()
+        for q in range(in_block):
+            to = b * in_block + q
+
+            @pl.when(r != to)
+            def _(to=to):
+                block_copy(ms, mr, m_send, m_recv, to, r).start()
 
     mr[r] = ms[r]
 
     @pl.loop(0, members)
     def _(k):
-        source = lax.rem(r + k, members)
+        source = lax.rem(r + members - k, members)
 
         @pl.when(k > 0)
         def _():
@@ -465,8 +477,8 @@
             vmem((lane_tiles, BLOCK, 3 * BLOCK), BF16),
             vmem((lane_tiles, *square), F32),
             vmem((lane_tiles, *square), F32),
-            vmem((MODES, width), F32),
-            vmem((look, MODES, width), F32),
+            vmem((MODES, width), BF16),
+            vmem((look, MODES, width), BF16),
             dma((6,)),
             dma((n_fsdp,)),
             dma((n_fsdp,)),

time: 53.9 us -> 50.9 us (0.944)
  the two profiles are of different devices: /device:TPU:61 before, /device:TPU:7 now
where the time goes in v3:
time: 50.9 us; the launch traced here: 50.6 us
  Pallas kernels  48.7 us (96%)
  local copies, waits for them, and re-layouts  1.87 us (4%)
    pallas_call x1, Pallas kernels, local(): pl.pallas_call(functools.partial(fused, n_ctx, n_fsdp, rows, look), out_s...  48.7 us
    unnamed x1, local copies, waits for them, and re-layouts  1.87 us

profile of v3, /device:TPU:7, one launch (start us, length us, event | category | flops | bytes accessed | tf_op | source)
XLA Modules:
  0.0 50.6 jit_solution(17075992078046500629)
XLA Ops:
  0.0 48.7 %shard_map.64 = bf16[32,8192]{1,0:T(8,128)(2,1)} custom-call(bf16[3,32,8192]{2,1,0:T(8,128)(2,1)} %streams.1, s32[128,128]{1,0:T(8,128)} %bitcast.4, f32[3,3,512]{2,1,0:T(4,128)} %taps.1, f32[16,32]{1,0:T(8,128)} %bitcast.5, f32[16,32]{1,0:T(8,128)} %bitcast.6, f32[4,128]{1,0:T(4,128)} %bitcast.7), custom_call_target="tpu_custom_call" | custom-call | tf_op jit(solution)/shard_map/pallas_call | solution.py:451
  48.7 1.9 %copy.8 = bf16[32,8192]{1,0:T(8,128)(2,1)} copy(bf16[32,8192]{1,0:T(8,128)(2,1)} %shard_map.64) | data formatting | bytes 1048576

commit v4 on v3

--- a/solution.py
+++ b/solution.py
@@ -37,8 +37,8 @@
 def fused(
     n_ctx, n_fsdp, rows, look,
     streams, segs, taps, decay, residue, skip, out,
-    x, hs, hb, hf, sg, own_taps, tp, dc, rs, sk, marks, gs, v, qs, ms, mr, inner, fresh, kc, cl, ri, dcy, carry, es, er,
-    in_sem, tap_send, tap_recv, halo_send, halo_recv, g_send, g_recv, e_send, e_recv, m_send, m_recv, hello, ready,
+    x, hs, hb, hf, sg, own_taps, tp, tq, dc, rs, sk, marks, gs, v, qs, ms, mr, inner, fresh, kc, cl, ri, dcy, carry, es, er,
+    in_sem, tap_send, tap_recv, tq_send, tq_recv, halo_send, halo_recv, g_send, g_recv, e_send, e_recv, m_send, m_recv, hello, ready,
 ):
     ctx, f = lax.axis_index("ctx"), lax.axis_index("fsdp")
     supers, members = n_ctx // 2, 2 * n_fsdp
@@ -57,11 +57,43 @@
     def at_super(step):
         return (ctx + 2 * step, f)
 
-    def tap_copy(owner, to):
+    chip, core = f // 2, lax.rem(f, 2)
+    chips = n_fsdp // 2
+
+    def tap_copy(buffer, sends, recvs, owner, to, slot):
         return pltpu.make_async_remote_copy(
-            src_ref=tp.at[owner], dst_ref=tp.at[owner], send_sem=tap_send.at[to],
-            recv_sem=tap_recv.at[owner], device_id=(ctx, to), device_id_type=MESH,
-        )
+            src_ref=buffer.at[owner], dst_ref=buffer.at[owner], send_sem=sends.at[slot],
+            recv_sem=recvs.at[owner], device_id=(ctx, to), device_id_type=MESH,
+        )
+
+    def kv_taps(owner, to, slot):
+        return tap_copy(tp, tap_send, tap_recv, owner, to, slot)
+
+    def query_taps(owner, to, slot):
+        return tap_copy(tq, tq_send, tq_recv, owner, to, slot)
+
+    partner = 2 * chip + 1 - core
+
+    def same_core(step):
+        return 2 * lax.rem(chip + step, chips) + core
+
+    def other_core(step):
+        return 2 * lax.rem(chip + step, chips) + 1 - core
+
+    def spread_taps(copy):
+        @pl.loop(1, chips)
+        def _(k):
+            copy(f, same_core(k), k).start()
+
+        copy(f, partner, 0).start()
+
+    def settle_taps(copy):
+        @pl.loop(1, chips)
+        def _(k):
+            copy(f, same_core(k), k).wait_send()
+            copy(same_core(chips - k), partner, chips + k).wait_send()
+
+        copy(f, partner, 0).wait_send()
 
     more = tile < supers - 1
     sends_halo = more | (r < members - 1)
@@ -79,13 +111,15 @@
             recv_sem=recvs.at[slot], device_id=member(to), device_id_type=MESH,
         )
 
-    def pass_ready(hop):
+    late = lax.rem(tile, max(supers // 2, 1)) == 0
+
+    def pass_ready(hop, now=True):
         if hop > look:
             return
-        known = tile + hop < supers
+        known = (tile + hop < supers) & now
         if hop == 1:
 
-            @pl.when(tile > 0)
+            @pl.when((tile > 0) & now)
             def _():
                 pl.semaphore_wait(hello, 1)
 
@@ -122,12 +156,6 @@
 
     barrier = pltpu.get_barrier_semaphore()
 
-    @pl.loop(1, members)
-    def _(k):
-        pl.semaphore_signal(
-            barrier, inc=1, device_id=member(lax.rem(r + k, members)), device_id_type=MESH
-        )
-
     @pl.when(tile > 0)
     def _():
         pl.semaphore_signal(barrier, inc=1, device_id=at_super(-1), device_id_type=MESH)
@@ -137,20 +165,30 @@
         pl.semaphore_signal(
             barrier, inc=1, device_id=(2 * tile - 1, n_fsdp - 1), device_id_type=MESH
         )
+
+    @pl.loop(0, members)
+    def _(k):
+        to = lax.rem(r + n_fsdp + k, members)
+
+        @pl.when(to != r)
+        def _():
+            pl.semaphore_signal(barrier, inc=1, device_id=member(to), device_id_type=MESH)
 
     loads[4].wait()
     for s in range(3):
         for j in range(3):
             for q in range(quads):
-                row = (s * 3 + j) * quads + q
-                tp[f, row : row + 1, :] = own_taps[s, j : j + 1, q * LANES : (q + 1) * LANES]
+                row = (max(s - 1, 0) * 3 + j) * quads + q
+                line = own_taps[s, j : j + 1, q * LANES : (q + 1) * LANES]
+                if s == 0:
+                    tq[f, row : row + 1, :] = line
+                else:
+                    tp[f, row : row + 1, :] = line
 
     greets = jnp.where(more, 1, 0) + jnp.where(more & (r == members - 1), 1, 0)
     pl.semaphore_wait(barrier, members - 1 + greets)
 
-    @pl.loop(1, n_fsdp)
-    def _(k):
-        tap_copy(f, lax.rem(f + k, n_fsdp)).start()
+    spread_taps(kv_taps)
 
     loads[5].wait()
     step = 4 * LANES
@@ -172,6 +210,8 @@
     @pl.when(more)
     def _():
         pl.semaphore_signal(hello, inc=1, device_id=at_super(1), device_id_type=MESH)
+
+    pass_ready(1, jnp.logical_not(late))
 
     for load in loads[:4]:
         load.wait()
@@ -236,7 +276,7 @@
     def _():
         hf[...] = jnp.zeros_like(hf)
 
-    pass_ready(1)
+    pass_ready(1, late)
 
     window = marks[pl.ds(pl.multiple_of(r * rows, rows), rows + 8), :]
     own_marks = window[8:]
@@ -252,41 +292,53 @@
         shift2 = jnp.where(row_id == 0, prev2, jnp.where(row_id == 1, prev1, pltpu.roll(now, 2, 0)))
 
         def tap(j):
-            row = (s * 3 + j) * quads + lane
-            return tp[owner, row : row + 1, :]
+            row = (max(s - 1, 0) * 3 + j) * quads + lane
+            return (tp if s else tq)[owner, pl.ds(row, 1), :]
 
         total = now * tap(0)
         total = total + jnp.where(agree[1], shift1, 0.0) * tap(1)
         return total + jnp.where(agree[2], shift2, 0.0) * tap(2)
 
+    def chunk_of(owner, lane):
+        chunk = owner * (2 * lane_tiles) + lane
+        return chunk, pl.ds(pl.multiple_of(chunk * LANES, LANES), LANES)
+
+    def send_gated(owner, part):
+        to = part * n_fsdp + owner
+        for m in range(lane_tiles):
+            lane = part * lane_tiles + m
+            chunk, _ = chunk_of(owner, lane)
+            gated = feature(1, owner, lane, chunk) * feature(2, owner, lane, chunk)
+            gs[to, :, m * LANES : (m + 1) * LANES] = gated.astype(BF16)
+
+        @pl.when(to != r)
+        def _():
+            block_copy(gs, v, g_send, g_recv, to, r).start()
+
+    far_half, near_half = 1 - half, half
+    send_gated(f, far_half)
+    pass_ready(2)
+
+    @pl.loop(1, chips)
+    def _(k):
+        owner = same_core(chips - k)
+        kv_taps(owner, partner, chips + k).wait_recv()
+        kv_taps(owner, partner, chips + k).start()
+        send_gated(owner, far_half)
+
+    pass_ready(3)
+
+    @pl.loop(0, chips)
+    def _(k):
+        owner = other_core(chips - k)
+        kv_taps(owner, f, 0).wait_recv()
+        send_gated(owner, far_half)
+
     @pl.loop(0, n_fsdp)
     def _(k):
-        owner = lax.rem(f + n_fsdp - k, n_fsdp)
-
-        @pl.when(k > 0)
-        def _():
-            tap_copy(owner, f).wait_recv()
-
-        for hop, point in ((2, n_fsdp // 4), (3, n_fsdp // 2)):
-
-            @pl.when(k == point)
-            def _(hop=hop):
-                pass_ready(hop)
-
-        for part in range(2):
-            to = part * n_fsdp + owner
-            for m in range(lane_tiles):
-                lane = part * lane_tiles + m
-                chunk = owner * (2 * lane_tiles) + lane
-                col = pl.ds(pl.multiple_of(chunk * LANES, LANES), LANES)
-                qs[:, col] = feature(0, owner, lane, chunk).astype(BF16)
-                gated = feature(1, owner, lane, chunk) * feature(2, owner, lane, chunk)
-                gs[to, :, m * LANES : (m + 1) * LANES] = gated.astype(BF16)
-
-            @pl.when(to != r)
-            def _():
-                block_copy(gs, v, g_send, g_recv, to, r).start()
-
+        send_gated(lax.rem(f + n_fsdp - k, n_fsdp), near_half)
+
+    spread_taps(query_taps)
     v[r] = gs[r]
 
     def marks_of(b):
@@ -327,7 +379,7 @@
         ).astype(BF16)
     for hop in range(4, look + 1):
         pass_ready(hop)
-    for d in range(1, look + 1):
+    for d in range(look, 0, -1):
 
         @pl.when(tile + d < supers)
         def _(d=d):
@@ -348,6 +400,50 @@
             gain = sk[pl.ds(half * lane_tiles + m, 1), :]
             inner[b, m] = direct + gain * vals.astype(F32)
 
+    @pl.loop(1, chips)
+    def _(k):
+        owner = same_core(chips - k)
+        query_taps(owner, partner, chips + k).wait_recv()
+        query_taps(owner, partner, chips + k).start()
+
+    def make_queries(owner):
+        for lane in range(2 * lane_tiles):
+            chunk, col = chunk_of(owner, lane)
+            qs[:, col] = feature(0, owner, lane, chunk).astype(BF16)
+
+    make_queries(f)
+
+    @pl.loop(1, chips)
+    def _(k):
+        make_queries(same_core(chips - k))
+
+    @pl.loop(0, chips)
+    def _(k):
+        owner = other_core(chips - k)
+        query_taps(owner, f, 0).wait_recv()
+        make_queries(owner)
+
+    def brought(m, state):
+        high, low = halves(state)
+        return jnp.dot(
+            ri[m], jnp.concatenate([high, high, low], axis=0), preferred_element_type=F32
+        )
+
+    for m in range(lane_tiles):
+        fade = jnp.exp(-dcy[m] * float(BLOCK))
+        state = fresh[0, m]
+        factor = jnp.ones(square, F32)
+        fresh[0, m] = factor
+        for b in range(1, blocks):
+            follow = (marks_of(b) == end_mark(b - 1)).astype(F32)
+            inner[b, m] += follow * brought(m, state)
+            if b < blocks - 1:
+                passing = (end_mark(b) == end_mark(b - 1)).astype(F32)
+                state = passing * fade * state + fresh[b, m]
+            passed = (end_mark(b - 1) == end_mark(b - 2)).astype(F32)
+            factor = passed * fade * factor
+            fresh[b, m] = factor
+
     first_mark = marks[8:9, :]
     for m in range(lane_tiles):
         carry[m] = jnp.zeros(square, F32)
@@ -365,27 +461,13 @@
                     part = part * jnp.exp(-dcy[m] * float(per * (d - 1)))
                 carry[m] += part
 
-    for m in range(lane_tiles):
-        state = carry[m]
-        fade = jnp.exp(-dcy[m] * float(BLOCK))
-        for b in range(blocks):
-            kept = fresh[b, m]
-            fresh[b, m] = state
-            if b < blocks - 1:
-                passing = (end_mark(b) == end_mark(b - 1)).astype(F32)
-                state = passing * fade * state + kept
-
     @pl.loop(0, blocks)
     def _(k):
-        b = lax.rem(r // in_block + k, blocks)
+        b = lax.rem(r // in_block + blocks // 2 + k, blocks)
         start = pl.multiple_of(b * BLOCK, BLOCK)
         follow = (marks[pl.ds(start + 8, BLOCK), :] == marks[pl.ds(start, 8), :][7:]).astype(F32)
         for m in range(lane_tiles):
-            high, low = halves(fresh[b, m])
-            brought = jnp.dot(
-                ri[m], jnp.concatenate([high, high, low], axis=0), preferred_element_type=F32
-            )
-            mixed = (inner[b, m] + follow * brought).astype(BF16)
+            mixed = (inner[b, m] + follow * brought(m, carry[m] * fresh[b, m])).astype(BF16)
             ms[pl.ds(b * in_block, in_block), :, m * LANES : (m + 1) * LANES] = mixed.reshape(
                 in_block, rows, LANES
             )
@@ -414,9 +496,8 @@
     def _():
         halo_copy().wait_send()
 
-    @pl.loop(1, n_fsdp)
-    def _(k):
-        tap_copy(f, lax.rem(f + k, n_fsdp)).wait_send()
+    settle_taps(kv_taps)
+    settle_taps(query_taps)
 
     @pl.loop(1, members)
     def _(k):
@@ -450,7 +531,7 @@
     vmem = pltpu.VMEM
     return pl.pallas_call(
         functools.partial(fused, n_ctx, n_fsdp, rows, look),
-        out_shape=jax.ShapeDtypeStruct((rows, model), BF16),
+        out_shape=vmem((rows, model), BF16),
         in_specs=[any_space] * 6,
         out_specs=pl.BlockSpec(memory_space=vmem),
         scratch_shapes=[
@@ -460,7 +541,8 @@
             vmem((8, model), F32),
             vmem(segs.shape, jnp.int32),
             vmem(short_taps.shape, F32),
-            vmem((n_fsdp, -(-9 * (short_taps.shape[2] // LANES) // 8) * 8, LANES), F32),
+            vmem((n_fsdp, 6 * (short_taps.shape[2] // LANES), LANES), F32),
+            vmem((n_fsdp, 4 * (short_taps.shape[2] // LANES), LANES), F32),
             vmem(rates.shape, F32),
             vmem(rates.shape, F32),
             vmem(skip.shape, F32),
@@ -482,6 +564,8 @@
             dma((6,)),
             dma((n_fsdp,)),
             dma((n_fsdp,)),
+            dma((n_fsdp,)),
+            dma((n_fsdp,)),
             dma(()),
             dma(()),
             dma((members,)),

time: 50.9 us -> 48.5 us (0.953)
  Pallas kernels: 48.7 us -> 47.2 us
  local copies, waits for them, and re-layouts: 1.87 us -> 0.8 us
    pallas_call x1, Pallas kernels: 48.7 us -> 47.2 us  [local(): pl.pallas_call(functools.partial(fused, n_ctx, n_fsdp, rows, look), out_s...]
    unnamed x1, local copies, waits for them, and re-layouts: 1.87 us -> 0.8 us
where the time goes in v4:
time: 48.5 us; the launch traced here: 48 us
  Pallas kernels  47.2 us (97%)
  local copies, waits for them, and re-layouts  0.8 us (2%)
    pallas_call x1, Pallas kernels, local(): pl.pallas_call(functools.partial(fused, n_ctx, n_fsdp, rows, look), out_s...  47.2 us

profile of v4, /device:TPU:7, one launch (start us, length us, event | category | flops | bytes accessed | tf_op | source)
XLA Modules:
  0.0 48.0 jit_solution(3563777656405844788)
XLA Ops:
  0.0 47.2 %shard_map.64 = bf16[32,8192]{1,0:T(8,128)(2,1)S(1)} custom-call(bf16[3,32,8192]{2,1,0:T(8,128)(2,1)} %streams.1, s32[128,128]{1,0:T(8,128)} %bitcast.4, f32[3,3,512]{2,1,0:T(4,128)} %taps.1, f32[16,32]{1,0:T(8,128)} %bitcast.5, f32[16,32]{1,0:T(8,128)} %bitcast.6, f32[4,128]{1,0:T(4,128)} %bitcast.7), custom_call_target="tpu_custom_call" | custom-call | tf_op jit(solution)/shard_map/pallas_call | solution.py:532
  47.2 0.8 %copy.8 = bf16[32,8192]{1,0:T(8,128)(2,1)} copy(bf16[32,8192]{1,0:T(8,128)(2,1)S(1)} %shard_map.64) | data formatting | bytes 1048576

commit v5 on v4

--- a/solution.py
+++ b/solution.py
@@ -37,7 +37,7 @@
 def fused(
     n_ctx, n_fsdp, rows, look,
     streams, segs, taps, decay, residue, skip, out,
-    x, hs, hb, hf, sg, own_taps, tp, tq, dc, rs, sk, marks, gs, v, qs, ms, mr, inner, fresh, kc, cl, ri, dcy, carry, es, er,
+    x, qhs, hs, qhb, hb, hf, sg, own_taps, tp, tq, dc, rs, sk, marks, gs, v, qs, ms, mr, inner, fresh, kc, cl, ri, dcy, carry, es, er,
     in_sem, tap_send, tap_recv, tq_send, tq_recv, halo_send, halo_recv, g_send, g_recv, e_send, e_recv, m_send, m_recv, hello, ready,
 ):
     ctx, f = lax.axis_index("ctx"), lax.axis_index("fsdp")
@@ -99,9 +99,10 @@
     sends_halo = more | (r < members - 1)
     gets_halo = (tile > 0) | (r > 0)
 
-    def halo_copy():
+    def halo_copy(part=1):
         return pltpu.make_async_remote_copy(
-            src_ref=hs, dst_ref=hb, send_sem=halo_send, recv_sem=halo_recv,
+            src_ref=hs if part else qhs, dst_ref=hb if part else qhb,
+            send_sem=halo_send.at[part], recv_sem=halo_recv.at[part],
             device_id=(2 * tile + (r + 1) // n_fsdp, lax.rem(f + 1, n_fsdp)), device_id_type=MESH,
         )
 
@@ -201,7 +202,8 @@
         for s in range(3):
             tail = x[s, rows - 8 : rows, col].astype(F32)
             total = jnp.where(slot == s, pltpu.roll(tail, 2 * s + 2, 0), total)
-        hs[:, col] = total.astype(BF16)
+        qhs[:, col] = total[:2].astype(BF16)
+        hs[:, col] = total[2:6].astype(BF16)
 
     @pl.when(sends_halo)
     def _():
@@ -270,7 +272,7 @@
     @pl.when(gets_halo)
     def _():
         halo_copy().wait_recv()
-        hf[...] = hb[...].astype(F32)
+        hf[2:6, :] = hb[...].astype(F32)
 
     @pl.when(jnp.logical_not(gets_halo))
     def _():
@@ -338,6 +340,10 @@
     def _(k):
         send_gated(lax.rem(f + n_fsdp - k, n_fsdp), near_half)
 
+    @pl.when(sends_halo)
+    def _():
+        halo_copy(0).start()
+
     spread_taps(query_taps)
     v[r] = gs[r]
 
@@ -354,16 +360,23 @@
         return four.reshape(BLOCK, LANES)
 
     spot = same_group.astype(F32)
-    for b in range(blocks):
-        for p in range(b * in_block, (b + 1) * in_block):
-
-            @pl.when(r != p)
-            def _(p=p):
-                block_copy(gs, v, g_send, g_recv, r, p).wait_recv()
-
-        ending = (marks_of(b) == end_mark(b)).astype(F32)
+
+    @pl.loop(0, blocks)
+    def _(k):
+        b = lax.rem(far_half * (blocks // 2) + k, blocks)
+        for q in range(in_block):
+            source = b * in_block + q
+
+            @pl.when(r != source)
+            def _(source=source):
+                block_copy(gs, v, g_send, g_recv, r, source).wait_recv()
+
+        start = pl.multiple_of(b * BLOCK, BLOCK)
+        its_end = marks[pl.ds(start + BLOCK, 8), :][7:]
+        ending = (marks[pl.ds(start + 8, BLOCK), :] == its_end).astype(F32)
         for m in range(lane_tiles):
-            kept = (values(b, m).astype(F32) * ending).astype(BF16)
+            four = v[pl.ds(b * in_block, in_block), :, m * LANES : (m + 1) * LANES]
+            kept = (four.reshape(BLOCK, LANES).astype(F32) * ending).astype(BF16)
             fresh[b, m] = spot * jnp.dot(
                 cl[m], jnp.concatenate([kept, kept], axis=0), preferred_element_type=F32
             )
@@ -410,6 +423,11 @@
         for lane in range(2 * lane_tiles):
             chunk, col = chunk_of(owner, lane)
             qs[:, col] = feature(0, owner, lane, chunk).astype(BF16)
+
+    @pl.when(gets_halo)
+    def _():
+        halo_copy(0).wait_recv()
+        hf[0:2, :] = qhb[...].astype(F32)
 
     make_queries(f)
 
@@ -482,9 +500,9 @@
 
     @pl.loop(0, members)
     def _(k):
-        source = lax.rem(r + members - k, members)
-
-        @pl.when(k > 0)
+        source = lax.rem(r + members + n_fsdp - k, members)
+
+        @pl.when(source != r)
         def _():
             block_copy(ms, mr, m_send, m_recv, r, source).wait_recv()
 
@@ -494,7 +512,8 @@
 
     @pl.when(sends_halo)
     def _():
-        halo_copy().wait_send()
+        halo_copy(0).wait_send()
+        halo_copy(1).wait_send()
 
     settle_taps(kv_taps)
     settle_taps(query_taps)
@@ -536,8 +555,10 @@
         out_specs=pl.BlockSpec(memory_space=vmem),
         scratch_shapes=[
             vmem((3, rows, model), BF16),
-            vmem((8, model), BF16),
-            vmem((8, model), BF16),
+            vmem((2, model), BF16),
+            vmem((4, model), BF16),
+            vmem((2, model), BF16),
+            vmem((4, model), BF16),
             vmem((8, model), F32),
             vmem(segs.shape, jnp.int32),
             vmem(short_taps.shape, F32),
@@ -566,8 +587,8 @@
             dma((n_fsdp,)),
             dma((n_fsdp,)),
             dma((n_fsdp,)),
-            dma(()),
-            dma(()),
+            dma((2,)),
+            dma((2,)),
             dma((members,)),
             dma((members,)),
             dma((look,)),

time: 48.5 us -> 48.5 us (level)
  no operation moved by 1% of the time
where the time goes in v5:
time: 48.5 us; the launch traced here: 48.3 us
  Pallas kernels  47.5 us (98%)
  local copies, waits for them, and re-layouts  0.8 us (2%)
    pallas_call x1, Pallas kernels, local(): pl.pallas_call(functools.partial(fused, n_ctx, n_fsdp, rows, look), out_s...  47.5 us

profile of v5, /device:TPU:7, one launch (start us, length us, event | category | flops | bytes accessed | tf_op | source)
XLA Modules:
  0.0 48.3 jit_solution(18239578864651019625)
XLA Ops:
  0.0 47.5 %shard_map.64 = bf16[32,8192]{1,0:T(8,128)(2,1)S(1)} custom-call(bf16[3,32,8192]{2,1,0:T(8,128)(2,1)} %streams.1, s32[128,128]{1,0:T(8,128)} %bitcast.4, f32[3,3,512]{2,1,0:T(4,128)} %taps.1, f32[16,32]{1,0:T(8,128)} %bitcast.5, f32[16,32]{1,0:T(8,128)} %bitcast.6, f32[4,128]{1,0:T(4,128)} %bitcast.7), custom_call_target="tpu_custom_call" | custom-call | tf_op jit(solution)/shard_map/pallas_call | solution.py:551
  47.6 0.8 %copy.8 = bf16[32,8192]{1,0:T(8,128)(2,1)} copy(bf16[32,8192]{1,0:T(8,128)(2,1)S(1)} %shard_map.64) | data formatting | bytes 1048576
